TPU v7x, 32 devices: a whole 2x2x4 slice. The times are simulated.
32 devices in a mesh: groups: 2 (over y), strip: 16 (over z, x, core).
Axes of the slice: x: 2, y: 2, z: 4, core: 2. Of those that a mesh axis runs over, the one named last changes fastest.
Arguments:
- bands: bfloat16 [64, 2048], P(('groups', 'strip')), parts along dimension 0, may hold values from -6 to 6
- target: bfloat16 [64, 2048], P('groups', 'strip'), parts along dimension 0, may hold values from -6 to 6
- w_in: bfloat16 [32, 128], replicated, may hold values from -1 to 1
- w_conv: bfloat16 [3, 3, 4, 32, 32], replicated, may hold values from -0.375 to 0.375
- w_track: bfloat16 [3, 3, 128, 128], replicated, may hold values from -0.3125 to 0.3125
- w_out: bfloat16 [128, 32], replicated, may hold values from -0.5 to 0.5
- table: float32 [64, 32], replicated, may hold values from -6 to 6
- dilation: int32 [3], replicated, may hold values from 1 to 8, as said below
- detector: int32 [128], P(('groups', 'strip')), parts along dimension 0, may hold values from 0 to 63
- flags: int32 [128], P(('groups', 'strip')), parts along dimension 0, may hold values 0 or 1
Outputs:
- prediction: bfloat16 [64, 2048], P('groups', 'strip'), parts along dimension 0
- grad_in: float32 [64, 128], P('groups'), parts along dimension 0
- grad_conv: float32 [6, 3, 4, 32, 32], P('groups'), parts along dimension 0
- grad_track: float32 [6, 3, 128, 128], P('groups'), parts along dimension 0
- grad_out: float32 [256, 32], P('groups'), parts along dimension 0
- grad_table: float32 [128, 32], P('groups'), parts along dimension 0
There are 2 independent parts, one for each index of `groups`. A program takes and returns all parts, laid end to end along the dimension named above; an argument that names none is the same for every part. Nothing has to cross between parts.
Inputs may be any that keep to these rules, and one draw needn't show every extreme that they name: `dilation`: each entry is 1 to 8, and one entry equals 8.
All inputs are finite; a program needn't handle non-finite values. No bound on the sum of `flags` on one device may be relied on, other than what follows from the above.
Results may differ from a plain program's by a relative error of at most 0.01.
Values may be sent and summed in bfloat16 or wider, within the bound.
No kernel may reach another device: no remote copies, remote signals or barrier semaphores. Data moves between devices by JAX's collectives and lax.ppermute only.
A program may use at most 64 MiB of HBM per device.

v0:
```python
import math

import jax
import jax.numpy as jnp
from jax import lax
from jax.sharding import PartitionSpec as P


def with_halo(x, sides, width):
    for axis, dim in sides:
        size, length = (lax.axis_size(axis), x.shape[dim])
        up = [(i, (i + 1) % size) for i in range(size - 1)]
        down = [(j, i) for i, j in up]
        last = lax.slice_in_dim(x, length - width, length, axis=dim)
        initial = lax.slice_in_dim(x, 0, width, axis=dim)
        before = lax.ppermute(last, axis, up)
        after = lax.ppermute(initial, axis, down)
        x = jnp.concatenate([before, x, after], axis=dim)
    return x


def silu_slope(preact):
    sigmoid_val = jax.nn.sigmoid(preact)
    return sigmoid_val * (1.0 + preact * (1.0 - sigmoid_val))


def block_diagonal(weight):
    groups = weight.shape[2]
    width = weight.shape[3]
    identity = jnp.eye(groups, dtype=weight.dtype)
    spread = weight[:, :, :, :, None, :] * identity[None, None, :, None, :, None]
    return spread.reshape(3, 3, groups * width, groups * width)


def conv_forward(padded, dense_weight):
    row_count = padded.shape[0] - 2
    col_count = padded.shape[1] - 2
    chan_count = padded.shape[2]
    summed = jnp.zeros((row_count * col_count, dense_weight.shape[3]), jnp.float32)
    for i in range(3):
        for j in range(3):
            window = padded[i : i + row_count, j : j + col_count].reshape(-1, chan_count)
            summed = summed + jnp.dot(
                window, dense_weight[i, j], preferred_element_type=jnp.float32
            )
    return summed.reshape(row_count, col_count, -1)


def conv_transpose(padded_grad, dense_weight):
    row_count = padded_grad.shape[0] - 2
    col_count = padded_grad.shape[1] - 2
    chan_count = padded_grad.shape[2]
    summed = jnp.zeros((row_count * col_count, dense_weight.shape[2]), jnp.float32)
    for i in range(3):
        for j in range(3):
            window = padded_grad[2 - i : 2 - i + row_count, 2 - j : 2 - j + col_count].reshape(
                -1, chan_count
            )
            summed = summed + jnp.dot(
                window, dense_weight[i, j].T, preferred_element_type=jnp.float32
            )
    return summed.reshape(row_count, col_count, -1)


def conv_weight_grad(padded, gradient, groups):
    row_count = gradient.shape[0]
    col_count = gradient.shape[1]
    chan_count = gradient.shape[2]
    width = chan_count // groups
    contract = (((0,), (0,)), ((), ()))
    flat_out = gradient.reshape(-1, chan_count)
    rows_of_taps = []
    for i in range(3):
        taps = []
        for j in range(3):
            window = padded[i : i + row_count, j : j + col_count].reshape(-1, chan_count)
            full = lax.dot_general(window, flat_out, contract, preferred_element_type=jnp.float32)
            taps.append(
                jnp.stack(
                    [
                        full[g * width : (g + 1) * width, g * width : (g + 1) * width]
                        for g in range(groups)
                    ]
                )
            )
        rows_of_taps.append(jnp.stack(taps))
    return jnp.stack(rows_of_taps)


def shifted(source, offset, margin):
    padded = jnp.pad(source, ((margin, margin), (0, 0), (0, 0)))
    return lax.dynamic_slice_in_dim(padded, margin + offset, source.shape[0], 0)


def project_pixels(pixels, w_in):
    flat = jnp.dot(pixels.reshape(-1, pixels.shape[2]), w_in, preferred_element_type=jnp.float32)
    return flat.astype(jnp.bfloat16).reshape(pixels.shape[0], pixels.shape[1], w_in.shape[1])


def column_work(
    features, target_block, w_track, w_out, table, dilation, detector, flags, loss_scale
):
    row_count, col_count, chan_count = features.shape
    band_count = w_out.shape[1]
    layers = w_track.shape[0]
    margin = row_count // 4
    contract = (((0,), (0,)), ((), ()))
    selector = (detector[:, None] == jnp.arange(table.shape[0], dtype=jnp.int32)[None, :]).astype(
        jnp.float32
    )
    flag_values = flags.astype(jnp.float32)
    offsets = flag_values[:, None] * jnp.dot(selector, table, precision=lax.Precision.HIGHEST)
    activations = [features]
    preacts = []
    current = features
    for layer_index in range(layers):
        spacing = dilation[layer_index]
        preact = jnp.zeros((row_count * col_count, chan_count), jnp.float32)
        for tap_index in range(3):
            moved_rows = shifted(current, (tap_index - 1) * spacing, margin)
            preact = preact + jnp.dot(
                moved_rows.reshape(-1, chan_count),
                w_track[layer_index, tap_index],
                preferred_element_type=jnp.float32,
            )
        preact = preact.reshape(row_count, col_count, chan_count)
        current = (current.astype(jnp.float32) + jax.nn.silu(preact)).astype(jnp.bfloat16)
        preacts.append(preact)
        activations.append(current)
    raw_output = (
        jnp.dot(current.reshape(-1, chan_count), w_out, preferred_element_type=jnp.float32).reshape(
            row_count, col_count, band_count
        )
        + offsets[None]
    )
    prediction = raw_output.astype(jnp.bfloat16)
    residue = (
        prediction.astype(jnp.float32)
        - target_block.reshape(row_count, col_count, band_count).astype(jnp.float32)
    ) * loss_scale
    residue_b = residue.astype(jnp.bfloat16)
    grad_out = lax.dot_general(
        current.reshape(-1, chan_count),
        residue_b.reshape(-1, band_count),
        contract,
        preferred_element_type=jnp.float32,
    )
    column_sums = jnp.sum(residue, axis=0) * flag_values[:, None]
    grad_table = jnp.dot(selector.T, column_sums, precision=lax.Precision.HIGHEST)
    backward = jnp.dot(
        residue_b.reshape(-1, band_count), w_out.T, preferred_element_type=jnp.float32
    ).reshape(row_count, col_count, chan_count)
    track_grads = [None] * layers
    for layer_index in reversed(range(layers)):
        spacing = dilation[layer_index]
        gate_grad = (backward * silu_slope(preacts[layer_index])).astype(jnp.bfloat16)
        flat_grad = gate_grad.reshape(-1, chan_count)
        tap_grads = []
        for tap_index in range(3):
            moved_rows = shifted(activations[layer_index], (tap_index - 1) * spacing, margin)
            tap_grads.append(
                lax.dot_general(
                    moved_rows.reshape(-1, chan_count),
                    flat_grad,
                    contract,
                    preferred_element_type=jnp.float32,
                )
            )
            pulled = jnp.dot(
                flat_grad, w_track[layer_index, tap_index].T, preferred_element_type=jnp.float32
            ).reshape(row_count, col_count, chan_count)
            backward = backward + shifted(pulled, (1 - tap_index) * spacing, margin)
        track_grads[layer_index] = jnp.stack(tap_grads)
    return (
        backward.astype(jnp.bfloat16),
        prediction.reshape(row_count, col_count * band_count),
        jnp.stack(track_grads),
        grad_out,
        grad_table,
    )


def body(bands, target, w_in, w_conv, w_track, w_out, table, dilation, detector, flags):
    band_count = w_in.shape[0]
    chan_count = w_in.shape[1]
    groups = w_conv.shape[2]
    device_count = lax.axis_size("strip")
    dense_conv = block_diagonal(w_conv)
    row_count = bands.shape[0]
    col_count = bands.shape[1] // band_count
    pixels = bands.reshape(row_count, col_count, band_count)
    projected = project_pixels(pixels, w_in)
    padded = with_halo(projected, (("strip", 0),), 1)
    padded = jnp.pad(padded, ((0, 0), (1, 1), (0, 0)))
    spatial = conv_forward(padded, dense_conv)
    features = (projected.astype(jnp.float32) + jax.nn.silu(spatial)).astype(jnp.bfloat16)
    feature_cols = lax.all_to_all(features, "strip", split_axis=1, concat_axis=0, tiled=True)
    loss_scale = 1.0 / math.sqrt(feature_cols.shape[0] * feature_cols.shape[1] * device_count)
    feature_grad, prediction, grad_track, grad_out, grad_table = column_work(
        feature_cols, target, w_track, w_out, table, dilation, detector, flags, loss_scale
    )
    local_grad = lax.all_to_all(feature_grad, "strip", split_axis=0, concat_axis=1, tiled=True)
    mixed_grad = (local_grad.astype(jnp.float32) * silu_slope(spatial)).astype(jnp.bfloat16)
    grad_pad = with_halo(mixed_grad, (("strip", 0),), 1)
    grad_pad = jnp.pad(grad_pad, ((0, 0), (1, 1), (0, 0)))
    lifted = (local_grad.astype(jnp.float32) + conv_transpose(grad_pad, dense_conv)).astype(
        jnp.bfloat16
    )
    grad_conv = conv_weight_grad(padded, mixed_grad, groups)
    contract = (((0,), (0,)), ((), ()))
    grad_in = lax.dot_general(
        pixels.reshape(-1, band_count),
        lifted.reshape(-1, chan_count),
        contract,
        preferred_element_type=jnp.float32,
    )
    grad_in, grad_conv, grad_track, grad_out, grad_table = lax.psum(
        (grad_in, grad_conv, grad_track, grad_out, grad_table), "strip"
    )
    return (prediction, grad_in, grad_conv, grad_track, grad_out, grad_table)


def solution(mesh):
    placed = (
        P(("groups", "strip"), None),
        P("groups", "strip"),
        P(),
        P(),
        P(),
        P(),
        P(),
        P(),
        P(("groups", "strip")),
        P(("groups", "strip")),
    )
    return jax.shard_map(
        body,
        mesh=mesh,
        in_specs=placed,
        out_specs=(
            P("groups", "strip"),
            P("groups", None),
            P("groups", None, None, None, None),
            P("groups", None, None, None),
            P("groups", None),
            P("groups", None),
        ),
        check_vma=False,
    )
```

profile of v0, /device:TPU:0, one launch (start us, length us, event | category | flops | bytes accessed | tf_op | source)
XLA Modules:
  0.0 162.6 jit_solution(9685957175195041190)
XLA Ops:
  7.2 0.8 reshape_reshape.4
  8.0 0.8 convolution_convert_fusion
  8.8 1.3 collective-permute-start.1
  10.1 3.0 %collective-permute-start = (bf16[1,64,128]{2,1,0:T(8,128)(2,1)S(1)}, bf16[1,64,128]{2,1,0:T(8,128)(2,1)S(1)}, u32[]{:S(2)}, u32[]{:S(2)}) collective-permute-start(bf16[1,64,128]{2,1,0:T(8,128)(2,1)S(1)} %get-tuple-element.73), channel_id=1, source_target_pairs={{0,1},{1,2},{2,3},{3,4},{4,5},{5,6},{6,7},{7,8},{8,9},{9,10},{10,1... | collective-permute-start | bytes 49160 | tf_op jit(solution)/shard_map/ppermute | solution.py:16
  13.2 0.7 convert_element_type.177
  13.8 1.5 mul.138
  15.3 0.6 mul.139
  17.8 0.6 copy.53
  18.5 8.0 %all-to-all-start = ((bf16[2,64,128]{2,0,1:T(2,128)(2,1)}), bf16[2,64,128]{2,0,1:T(2,128)(2,1)S(1)}, u32[]{:S(2)}, u32[]{:S(2)}) async-start(bf16[2,64,128]{2,0,1:T(2,128)(2,1)} %copy.53), calls=%async_computation | async-start | bytes 65536 | tf_op jit(solution)/shard_map/all_to_all | solution.py:197
  26.4 0.6 fusion.102
  35.4 0.2 multiply_convert_fusion.3
  35.9 0.2 multiply_convert_fusion.2
  36.4 0.2 convolution_bitcast_fusion.18
  38.3 0.6 copy.73
  38.9 6.0 %all-to-all-start.1 = ((bf16[32,4,128]{2,1,0:T(4,128)(2,1)}), bf16[32,4,128]{2,1,0:T(4,128)(2,1)S(1)}, u32[]{:S(2)}, u32[]{:S(2)}) async-start(bf16[32,4,128]{2,1,0:T(4,128)(2,1)} %copy.73), calls=%async_computation.1 | async-start | bytes 65536 | tf_op jit(solution)/shard_map/all_to_all | solution.py:202
  44.9 0.3 fusion.80
  45.2 0.2 convolution_bitcast_fusion.9
  45.5 0.9 pad_maximum_fusion.1
  46.3 0.7 reshape.252
  47.0 4.5 %all-to-all-done.1 = bf16[32,4,128]{2,1,0:T(4,128)(2,1)S(1)} async-done(((bf16[32,4,128]{2,1,0:T(4,128)(2,1)}), bf16[32,4,128]{2,1,0:T(4,128)(2,1)S(1)}, u32[]{:S(2)}, u32[]{:S(2)}) %all-to-all-start.1) | async-done | bytes 32800 | tf_op jit(solution)/shard_map/all_to_all | solution.py:202
  51.6 0.2 convolution_bitcast_fusion.11
  52.0 0.2 convolution_bitcast_fusion.13
  52.7 1.3 collective-permute-start.3
  54.0 3.0 %collective-permute-start.2 = (bf16[1,64,128]{2,1,0:T(8,128)(2,1)S(1)}, bf16[1,64,128]{2,1,0:T(8,128)(2,1)S(1)}, u32[]{:S(2)}, u32[]{:S(2)}) collective-permute-start(bf16[1,64,128]{2,1,0:T(8,128)(2,1)S(1)} %get-tuple-element.61), channel_id=1, source_target_pairs={{0,1},{1,2},{2,3},{3,4},{4,5},{5,6},{6,7},{7,8},{8,9},{9,10},{10,1... | collective-permute-start | bytes 49160 | tf_op jit(solution)/shard_map/ppermute | solution.py:16
  57.2 0.2 convolution_bitcast_fusion
  58.2 0.2 convolution_bitcast_fusion.1
  58.6 0.9 pad_maximum_fusion
  60.8 0.3 fusion.10
  61.2 59.5 %all-reduce.11 = (f32[32,128]{1,0:T(8,128)}, f32[128,32]{0,1:T(8,128)}, f32[64,32]{0,1:T(8,128)}) all-reduce(f32[32,128]{1,0:T(8,128)S(1)} %fusion.10, f32[128,32]{0,1:T(8,128)S(1)} %convolution_bitcast_fusion.18, f32[64,32]{0,1:T(8,128)S(1)} %fusion.80), channel_id=1, replica_groups=mesh['groups'=2,'strip'=16] {'strip'}, use_global_device_ids=true, to_apply=%region_0.1 | all-reduce | flops 10240 | bytes 81920 | tf_op jit(solution)/shard_map/psum | solution.py:217
  120.7 32.3 %all-reduce.15.cloned.1.call-done = (f32[3,3,4,32,32]{4,3,2,1,0:T(8,128)}, f32[3,3,128,128]{3,2,1,0:T(8,128)}) async-done(((f32[3,3,4,32,32]{4,3,2,1,0:T(8,128)}, f32[3,3,128,128]{3,2,1,0:T(8,128)}), (f32[3,3,4,32,32]{4,3,2,1,0:T(8,128)}, f32[3,3,128,128]{3,2,1,0:T(8,128)})) %all-reduce.15.cloned.1.call-update) | async-done | bytes 737296 | tf_op jit(solution)/shard_map/psum | solution.py:217
  152.9 2.0 %copy.107 = f32[3,3,4,32,32]{4,3,2,1,0:T(8,128)} copy(f32[3,3,4,32,32]{4,3,2,1,0:T(8,128)} %get-tuple-element.100) | data formatting | bytes 294912
  154.9 0.8 copy.108
  (122 shorter events, 9.7 us)
Async XLA Ops:
  7.2 9.0 %copy-start = (f32[64,32]{0,1:T(8,128)S(1)}, f32[64,32]{0,1:T(8,128)}, u32[]{:S(2)}) copy-start(f32[64,32]{0,1:T(8,128)} %param.16) | copy-start | bytes 24580
  8.8 7.6 %collective-permute-start.1 = (bf16[1,64,128]{2,1,0:T(8,128)(2,1)S(1)}, bf16[1,64,128]{2,1,0:T(8,128)(2,1)S(1)}, u32[]{:S(2)}, u32[]{:S(2)}) collective-permute-start(bf16[1,64,128]{2,1,0:T(8,128)(2,1)S(1)} %get-tuple-element.74), channel_id=1, source_target_pairs={{1,0},{2,1},{3,2},{4,3},{5,4},{6,5},{7,6},{8,7},{9,8},{10,9},{11,1... | collective-permute-start | bytes 49160 | tf_op jit(solution)/shard_map/ppermute | solution.py:17
  10.1 6.3 %collective-permute-start = (bf16[1,64,128]{2,1,0:T(8,128)(2,1)S(1)}, bf16[1,64,128]{2,1,0:T(8,128)(2,1)S(1)}, u32[]{:S(2)}, u32[]{:S(2)}) collective-permute-start(bf16[1,64,128]{2,1,0:T(8,128)(2,1)S(1)} %get-tuple-element.73), channel_id=1, source_target_pairs={{0,1},{1,2},{2,3},{3,4},{4,5},{5,6},{6,7},{7,8},{8,9},{9,10},{10,1... | collective-permute-start | bytes 49160 | tf_op jit(solution)/shard_map/ppermute | solution.py:16
  15.3 0.9 copy-start.6
  16.4 10.0 %copy-start.5 = (s32[3]{0:T(128)S(1)}, s32[3]{0:T(128)}, u32[]{:S(2)}) copy-start(s32[3]{0:T(128)} %param.17) | copy-start | bytes 40
  16.5 16.4 %copy-start.3 = (bf16[32,128]{1,0:T(8,128)(2,1)S(1)}, bf16[32,128]{1,0:T(8,128)(2,1)}, u32[]{:S(2)}) copy-start(bf16[32,128]{1,0:T(8,128)(2,1)} %param.11) | copy-start | bytes 24580
  16.8 16.5 %copy-start.1 = (bf16[3,3,128,128]{3,2,1,0:T(8,128)(2,1)S(1)}, bf16[3,3,128,128]{3,2,1,0:T(8,128)(2,1)}, u32[]{:S(2)}) copy-start(bf16[3,3,128,128]{3,2,1,0:T(8,128)(2,1)} %param.14) | copy-start | bytes 884740
  18.5 14.6 %all-to-all-start = ((bf16[2,64,128]{2,0,1:T(2,128)(2,1)}), bf16[2,64,128]{2,0,1:T(2,128)(2,1)S(1)}, u32[]{:S(2)}, u32[]{:S(2)}) async-start(bf16[2,64,128]{2,0,1:T(2,128)(2,1)} %copy.53), calls=%async_computation | async-start | bytes 65536 | tf_op jit(solution)/shard_map/all_to_all | solution.py:197
  33.8 1.1 copy-start.4
  38.9 12.6 %all-to-all-start.1 = ((bf16[32,4,128]{2,1,0:T(4,128)(2,1)}), bf16[32,4,128]{2,1,0:T(4,128)(2,1)S(1)}, u32[]{:S(2)}, u32[]{:S(2)}) async-start(bf16[32,4,128]{2,1,0:T(4,128)(2,1)} %copy.73), calls=%async_computation.1 | async-start | bytes 65536 | tf_op jit(solution)/shard_map/all_to_all | solution.py:202
  44.9 108.0 %all-reduce.15.cloned.1.call-start = ((), (), s32[]{:S(2)}) async-start(), calls=%async_computation.2 | async-start | bytes 2359296 | tf_op jit(solution)/shard_map/psum | solution.py:217
  52.7 6.8 %collective-permute-start.3 = (bf16[1,64,128]{2,1,0:T(8,128)(2,1)S(1)}, bf16[1,64,128]{2,1,0:T(8,128)(2,1)S(1)}, u32[]{:S(2)}, u32[]{:S(2)}) collective-permute-start(bf16[1,64,128]{2,1,0:T(8,128)(2,1)S(1)} %get-tuple-element.62), channel_id=1, source_target_pairs={{1,0},{2,1},{3,2},{4,3},{5,4},{6,5},{7,6},{8,7},{9,8},{10,9},{11,1... | collective-permute-start | bytes 49160 | tf_op jit(solution)/shard_map/ppermute | solution.py:17
  54.0 5.5 %collective-permute-start.2 = (bf16[1,64,128]{2,1,0:T(8,128)(2,1)S(1)}, bf16[1,64,128]{2,1,0:T(8,128)(2,1)S(1)}, u32[]{:S(2)}, u32[]{:S(2)}) collective-permute-start(bf16[1,64,128]{2,1,0:T(8,128)(2,1)S(1)} %get-tuple-element.61), channel_id=1, source_target_pairs={{0,1},{1,2},{2,3},{3,4},{4,5},{5,6},{6,7},{7,8},{8,9},{9,10},{10,1... | collective-permute-start | bytes 49160 | tf_op jit(solution)/shard_map/ppermute | solution.py:16
  152.9 2.0 %copy-start.2 = (f32[3,3,128,128]{3,2,1,0:T(8,128)S(1)}, f32[3,3,128,128]{3,2,1,0:T(8,128)}, u32[]{:S(2)}) copy-start(f32[3,3,128,128]{3,2,1,0:T(8,128)} %get-tuple-element.101) | copy-start | bytes 1769476
Sparse Core Ops, SparseCore 0:
  59.6 93.2 all-reduce.14
where the time goes:
time: 163 us
  blocking collectives  59.5 us (37%)
  waiting for transfers between devices  36.8 us (23%)
  starting transfers between devices  22.6 us (14%)
  between operations  20.5 us (13%)
  matrix products  10.5 us (6%)
  local copies, waits for them, and re-layouts  9.7 us (6%)
  other arithmetic  2.92 us (2%)
    psum x1, blocking collectives, body(): lax.psum((grad_in, grad_conv, grad_track, grad_out, grad_table), 'strip')  59.5 us
    psum x1, waiting for transfers between devices, body(): lax.psum((grad_in, grad_conv, grad_track, grad_out, grad_table), 'strip')  32.3 us
    all_to_all x1, starting transfers between devices, body(): lax.all_to_all(features, 'strip', split_axis=1, concat_axis=0, tiled=True)  7.95 us
    ppermute x2, starting transfers between devices, with_halo(): before = lax.ppermute(last, axis, up)  6.06 us
    all_to_all x1, starting transfers between devices, body(): lax.all_to_all(feature_grad, 'strip', split_axis=0, concat_axis=1, tiled=...  5.97 us
    all_to_all x1, waiting for transfers between devices, body(): lax.all_to_all(feature_grad, 'strip', split_axis=0, concat_axis=1, tiled=...  4.5 us
  transfers between devices with their start and end apart: 7, of which 2 were waited for; matrix products, arithmetic and copies ran while one was open for 6% of the time, Pallas kernels for 0%

commit v1 on v0

--- a/solution.py
+++ b/solution.py
@@ -3,7 +3,11 @@
 import jax
 import jax.numpy as jnp
 from jax import lax
+from jax.experimental import pallas as pl
+from jax.experimental.pallas import tpu as pltpu
 from jax.sharding import PartitionSpec as P
+
+INTERPRET = False
 
 
 def with_halo(x, sides, width):
@@ -180,7 +184,7 @@
     )
 
 
-def body(bands, target, w_in, w_conv, w_track, w_out, table, dilation, detector, flags):
+def body_distributed(bands, target, w_in, w_conv, w_track, w_out, table, dilation, detector, flags):
     band_count = w_in.shape[0]
     chan_count = w_in.shape[1]
     groups = w_conv.shape[2]
@@ -220,6 +224,468 @@
     return (prediction, grad_in, grad_conv, grad_track, grad_out, grad_table)
 
 
+LANES = 128
+HALF = 64
+SLOTS = 4
+VMEM_BUDGET = 48 * 1024 * 1024
+
+
+def low_half(shape):
+    return lax.broadcasted_iota(jnp.int32, shape, len(shape) - 1) % LANES < HALF
+
+
+def swap_halves(x):
+    return pltpu.roll(x, HALF, 1)
+
+
+def expand_tap(weight):
+    turned = swap_halves(weight)
+    low = low_half((HALF, LANES))
+    zero = jnp.zeros((HALF, LANES), jnp.float32)
+    blocks = []
+    for h in range(2):
+        own = weight[h * HALF : (h + 1) * HALF]
+        other = turned[h * HALF : (h + 1) * HALF]
+        blocks.append(jnp.concatenate([jnp.where(low, own, zero), jnp.where(low, other, zero)], axis=1))
+        blocks.append(jnp.concatenate([jnp.where(low, zero, other), jnp.where(low, zero, own)], axis=1))
+    return jnp.concatenate(blocks, axis=0)
+
+
+def expand_band(weight):
+    band_count = weight.shape[0]
+    turned = swap_halves(weight)
+    low = low_half((band_count, LANES))
+    zero = jnp.zeros((band_count, LANES), jnp.float32)
+    columns = []
+    for h in range(2):
+        first, second = (weight, turned) if h == 0 else (turned, weight)
+        for pair in range(2):
+            rows = [zero] * SLOTS
+            rows[2 * pair] = jnp.where(low, first, zero)
+            rows[2 * pair + 1] = jnp.where(low, zero, second)
+            columns.append(jnp.concatenate(rows, axis=0))
+    return jnp.concatenate(columns, axis=1)
+
+
+INPUT_SLOTS = (0, 1, 2, 3, 4, -1)
+
+
+def expand_conv(taps, ref, transposed):
+    width = taps.shape[0] // 9
+    low = low_half((HALF, LANES))
+    zero = jnp.zeros((HALF, LANES), jnp.float32)
+    row = lax.broadcasted_iota(jnp.int32, (HALF, LANES), 0) // width
+    lane = lax.broadcasted_iota(jnp.int32, (HALF, LANES), 1) // width % 2
+    same = row == lane
+    for i in range(3):
+        for h in range(2):
+            values = []
+            for j in range(3):
+                tap = taps[(3 * i + j) * width : (3 * i + j + 1) * width]
+                turned = swap_halves(tap)
+                spread = jnp.where(low[:width], tap, turned) if h == 0 else jnp.where(low[:width], turned, tap)
+                values.append(jnp.where(same, jnp.concatenate([spread, spread], axis=0), zero))
+            place = 2 - i if transposed else i
+            for position, slot in enumerate(INPUT_SLOTS):
+                tiles = []
+                for pair in range(2):
+                    pieces = []
+                    for half in range(2):
+                        out_slot = 2 * pair + half
+                        j = out_slot + 1 - slot if transposed else slot - out_slot + 1
+                        pieces.append(values[j] if 0 <= j <= 2 else zero)
+                    tiles.append(jnp.where(low, pieces[0], pieces[1]))
+                start = (place * len(INPUT_SLOTS) + position) * HALF
+                ref[h, start : start + HALF, :] = jnp.concatenate(tiles, axis=1).astype(ref.dtype)
+
+
+def prepare_kernel(w_in, w_out_t, taps, taps_t, w_track, w4, wo4, wc, wt, wf, wb):
+    w4[...] = expand_band(w_in[...].astype(jnp.float32)).astype(w4.dtype)
+    wo4[...] = expand_band(w_out_t[...].astype(jnp.float32)).astype(wo4.dtype)
+    expand_conv(taps[...].astype(jnp.float32), wc, False)
+    expand_conv(taps_t[...].astype(jnp.float32), wt, True)
+    layers = w_track.shape[0]
+    for layer in range(layers):
+        for tap in range(3):
+            weight = w_track[layer, tap].astype(jnp.float32)
+            rows = pl.ds(tap * 2 * LANES, 2 * LANES)
+            wf[layer, rows, :] = expand_tap(weight).astype(wf.dtype)
+            wb[layer, rows, :] = expand_tap(weight.T).astype(wb.dtype)
+
+
+def prepare_weights(w_in, w_conv, w_track, w_out):
+    chan_count = w_in.shape[1]
+    width = w_conv.shape[3]
+    layers = w_track.shape[0]
+    taps = jnp.transpose(w_conv, (0, 1, 3, 2, 4)).reshape(9 * width, chan_count)
+    taps_t = jnp.transpose(w_conv, (0, 1, 4, 2, 3)).reshape(9 * width, chan_count)
+    shapes = (
+        (SLOTS * w_in.shape[0], SLOTS * chan_count),
+        (SLOTS * w_out.shape[1], SLOTS * chan_count),
+        (2, 18 * HALF, 2 * LANES),
+        (2, 18 * HALF, 2 * LANES),
+        (layers, 6 * LANES, 2 * LANES),
+        (layers, 6 * LANES, 2 * LANES),
+    )
+    return pl.pallas_call(
+        prepare_kernel,
+        out_shape=tuple(jax.ShapeDtypeStruct(s, jnp.bfloat16) for s in shapes),
+        interpret=INTERPRET,
+        name="prepare_weights",
+    )(w_in, w_out.T, taps, taps_t, w_track)
+
+
+def silu_and_slope(v):
+    s = 0.5 * jnp.tanh(0.5 * v) + 0.5
+    return v * s, s * (1.0 + v * (1.0 - s))
+
+
+def dot(a, b):
+    return jnp.dot(a, b, preferred_element_type=jnp.float32)
+
+
+def dot_tn(a, b):
+    return lax.dot_general(a, b, (((0,), (0,)), ((), ())), preferred_element_type=jnp.float32)
+
+
+def dot_nt(a, b):
+    return lax.dot_general(a, b, (((1,), (1,)), ((), ())), preferred_element_type=jnp.float32)
+
+
+def thirds(x):
+    first = x.astype(jnp.bfloat16)
+    rest = x - first.astype(jnp.float32)
+    second = rest.astype(jnp.bfloat16)
+    third = (rest - second.astype(jnp.float32)).astype(jnp.bfloat16)
+    return first, second, third
+
+
+def band_diagonal(full):
+    rows = full.shape[0] // SLOTS
+    low = low_half((rows, LANES))
+    straight, crossed = None, None
+    for pair in range(2):
+        even = [full[2 * pair * rows : (2 * pair + 1) * rows, (2 * h + pair) * LANES : (2 * h + pair + 1) * LANES] for h in range(2)]
+        odd = [full[(2 * pair + 1) * rows : (2 * pair + 2) * rows, (2 * h + pair) * LANES : (2 * h + pair + 1) * LANES] for h in range(2)]
+        direct = jnp.where(low, even[0], odd[1])
+        swapped = jnp.where(low, even[1], odd[0])
+        straight = direct if straight is None else straight + direct
+        crossed = swapped if crossed is None else crossed + swapped
+    return straight + swap_halves(crossed)
+
+
+def step_kernel(
+    rows_total,
+    blocks,
+    margin,
+    loss_scale,
+    own,
+    dilation,
+    gathered,
+    w4,
+    wo4,
+    wc,
+    wt,
+    wf,
+    wb,
+    table_t,
+    prediction,
+    grad_in,
+    grad_conv,
+    grad_track,
+    grad_out_t,
+    grad_table_t,
+    pixels,
+    target,
+    meta,
+    proj,
+    mixed,
+    acts,
+    gates,
+    slopes,
+    backward,
+    shown,
+):
+    size = rows_total * blocks
+    strips = gathered.shape[0]
+    rows_local = rows_total // strips
+    layers = wf.shape[0]
+    bf16 = jnp.bfloat16
+    f32 = jnp.float32
+    mine = own[0]
+    bits = strips.bit_length() - 1
+    local = rows_local * blocks
+    middle = pl.ds(margin * blocks, size)
+
+    for s in range(strips):
+        apart = mine ^ s
+        place = 0
+        for b in range(bits):
+            place = place * 2 + ((apart >> b) & 1)
+        pixels[s * local : (s + 1) * local, :] = gathered[place, 0:local, :]
+        target[pl.ds(s, rows_total, stride=blocks), :] = gathered[place, local : local + rows_total, :].astype(f32)
+        meta[s : s + 1, :] = gathered[place, local + rows_total : local + rows_total + 16, :].astype(f32)[0:1]
+
+    for ref in (proj, mixed):
+        ref[0:blocks, :] = jnp.zeros((blocks, ref.shape[1]), bf16)
+        ref[size + blocks : size + 2 * blocks, :] = jnp.zeros((blocks, ref.shape[1]), bf16)
+    edge = jnp.zeros((margin * blocks, acts.shape[2]), bf16)
+    for layer in range(layers):
+        acts[layer, 0 : margin * blocks, :] = edge
+        acts[layer, margin * blocks + size :, :] = edge
+    gates[0 : margin * blocks, :] = edge
+    gates[margin * blocks + size :, :] = edge
+
+    low = low_half((size, LANES))
+    position = lax.broadcasted_iota(jnp.int32, (size, LANES), 0) % blocks
+    outside = jnp.where(low, blocks - 1, 0)
+    keep = position != outside
+
+    def put_padded(ref, value):
+        rounded = value.astype(bf16)
+        ref[blocks : blocks + size, 0 : 4 * LANES] = rounded
+        wide = rounded.astype(f32)
+        for h in range(2):
+            following = pltpu.roll(wide[:, 2 * h * LANES : (2 * h + 1) * LANES], size - 1, 0)
+            previous = pltpu.roll(wide[:, (2 * h + 1) * LANES : (2 * h + 2) * LANES], 1, 0)
+            side = jnp.where(keep, jnp.where(low, following, previous), 0.0)
+            ref[blocks : blocks + size, (4 + h) * LANES : (5 + h) * LANES] = side.astype(bf16)
+
+    def window(ref, h, i):
+        rows = slice(i * blocks, i * blocks + size)
+        return [ref[rows, 2 * h * LANES : (2 * h + 2) * LANES], ref[rows, (4 + h) * LANES : (5 + h) * LANES]]
+
+    put_padded(proj, dot(pixels[...], w4[...]))
+    for h in range(2):
+        lanes = slice(2 * h * LANES, (2 * h + 2) * LANES)
+        left = jnp.concatenate([piece for i in range(3) for piece in window(proj, h, i)], axis=1)
+        silu, slope = silu_and_slope(dot(left, wc[h]))
+        slopes[layers, :, lanes] = slope
+        centre = proj[blocks : blocks + size, lanes].astype(f32)
+        acts[0, middle, lanes] = (centre + silu).astype(bf16)
+
+    def tap_window(ref, spacing, sign, pair):
+        pieces = []
+        for tap in range(3):
+            start = pl.multiple_of((margin + sign * (tap - 1) * spacing) * blocks, 16)
+            for h in range(2):
+                pieces.append(ref[pl.ds(start, size), (2 * h + pair) * LANES : (2 * h + pair + 1) * LANES])
+        return jnp.concatenate(pieces, axis=1)
+
+    def forward(layer, carry):
+        spacing = dilation[layer]
+        for pair in range(2):
+            silu, slope = silu_and_slope(dot(tap_window(acts.at[layer], spacing, 1, pair), wf[layer]))
+            for h in range(2):
+                lanes = slice((2 * h + pair) * LANES, (2 * h + pair + 1) * LANES)
+                part = slice(h * LANES, (h + 1) * LANES)
+                slopes[layer, :, lanes] = slope[:, part]
+                centre = acts[layer, middle, lanes].astype(f32)
+                acts[layer + 1, middle, lanes] = (centre + silu[:, part]).astype(bf16)
+        return carry
+
+    lax.fori_loop(0, layers, forward, 0)
+
+    det_count = table_t.shape[1] // SLOTS
+    meta_b = meta[...].astype(bf16)
+    source = lax.broadcasted_iota(jnp.int32, (LANES, SLOTS * det_count), 0)
+    slot_of = lax.broadcasted_iota(jnp.int32, (LANES, SLOTS * det_count), 1) // det_count
+    spread = jnp.where(source == slot_of, 1.0, jnp.where(source == slot_of + SLOTS, 256.0, 0.0)).astype(bf16)
+    element = (lax.broadcasted_iota(jnp.int32, (blocks, SLOTS * det_count), 1) % det_count).astype(f32)
+    selector = jnp.where(dot(meta_b, spread) == element, 1.0, 0.0).astype(bf16)
+    source = lax.broadcasted_iota(jnp.int32, (LANES, LANES), 0)
+    slot_of = lax.broadcasted_iota(jnp.int32, (LANES, LANES), 1) // (LANES // SLOTS)
+    flag = dot(meta_b, jnp.where(source == slot_of + 2 * SLOTS, 1.0, 0.0).astype(bf16))
+    offsets = sum(dot_nt(selector, part) for part in thirds(table_t[...])) * flag
+
+    raw = dot_nt(acts[layers, middle, :], wo4[...]).reshape(rows_total, blocks, LANES) + offsets[None]
+    rounded = raw.astype(bf16).astype(f32)
+    shown[...] = rounded.reshape(size, LANES)
+    prediction[...] = shown[pl.ds(mine, rows_total, stride=blocks), :].astype(bf16)
+    residue = (rounded - target[...].reshape(rows_total, blocks, LANES)) * loss_scale
+    column_sums = jnp.sum(residue, axis=0) * flag
+    residue_b = residue.reshape(size, LANES).astype(bf16)
+    backward[...] = dot(residue_b, wo4[...])
+    grad_out_t[...] = band_diagonal(dot_tn(residue_b, acts[layers, middle, :]))
+    sums = jnp.concatenate(thirds(column_sums), axis=0)
+    full = dot_tn(sums, jnp.concatenate([selector] * 3, axis=0))
+    band_count = LANES // SLOTS
+    grad_table_t[...] = sum(
+        full[k * band_count : (k + 1) * band_count, k * det_count : (k + 1) * det_count] for k in range(SLOTS)
+    )
+
+    tap_low = low_half((HALF, LANES))
+
+    def back(step, carry):
+        layer = layers - 1 - step
+        spacing = dilation[layer]
+        gates[middle, :] = (backward[...] * slopes[layer]).astype(bf16)
+        moved = []
+        for pair in range(2):
+            right = tap_window(gates, spacing, -1, pair)
+            moved.append(right)
+            update = dot(right, wb[layer])
+            for h in range(2):
+                lanes = slice((2 * h + pair) * LANES, (2 * h + pair + 1) * LANES)
+                backward[:, lanes] = backward[:, lanes] + update[:, h * LANES : (h + 1) * LANES]
+        left = [
+            jnp.concatenate(
+                [acts[layer, middle, (2 * h + pair) * LANES : (2 * h + pair + 1) * LANES] for h in range(2)], axis=1
+            )
+            for pair in range(2)
+        ]
+        full = dot_tn(jnp.concatenate(left, axis=0), jnp.concatenate(moved, axis=0))
+        for tap in range(3):
+            first = full[:, 2 * tap * LANES : (2 * tap + 1) * LANES]
+            second = full[:, (2 * tap + 1) * LANES : (2 * tap + 2) * LANES]
+            for h in range(2):
+                upper = slice(2 * h * HALF, (2 * h + 1) * HALF)
+                lower = slice((2 * h + 1) * HALF, (2 * h + 2) * HALF)
+                straight = jnp.where(tap_low, first[upper], second[lower])
+                crossed = jnp.where(tap_low, second[upper], first[lower])
+                start = pl.multiple_of((layer * 3 + tap) * LANES, LANES) + h * HALF
+                grad_track[pl.ds(start, HALF), :] = straight + swap_halves(crossed)
+        return carry
+
+    lax.fori_loop(0, layers, back, 0)
+
+    feature_grad = backward[...].astype(bf16).astype(f32)
+    put_padded(mixed, feature_grad * slopes[layers])
+    lifted = []
+    for h in range(2):
+        lanes = slice(2 * h * LANES, (2 * h + 2) * LANES)
+        left = jnp.concatenate([piece for i in range(3) for piece in window(mixed, h, i)], axis=1)
+        lifted.append((backward[:, lanes].astype(bf16).astype(f32) + dot(left, wt[h])).astype(bf16))
+    grad_in[...] = band_diagonal(dot_tn(pixels[...], jnp.concatenate(lifted, axis=1)))
+
+    width = grad_conv.shape[1]
+    for h in range(2):
+        left = jnp.concatenate(window(proj, h, 1), axis=1)
+        right = jnp.concatenate(
+            [mixed[(2 - i) * blocks : (2 - i) * blocks + size, 2 * h * LANES : (2 * h + 2) * LANES] for i in range(3)],
+            axis=1,
+        )
+        full = dot_tn(left, right)
+        for i in range(3):
+            for j in range(3):
+                parts = []
+                for out_slot in range(SLOTS):
+                    row = INPUT_SLOTS.index(out_slot + j - 1) * HALF
+                    tile = 2 * i + out_slot // 2
+                    parts.append(full[row : row + HALF, tile * LANES : (tile + 1) * LANES])
+                total = parts[0] + parts[2] + swap_halves(parts[1] + parts[3])
+                for g in range(2):
+                    start = ((3 * i + j) * 4 + 2 * h + g) * width
+                    piece = total[g * width : (g + 1) * width]
+                    if g:
+                        piece = pltpu.roll(piece, LANES - width, 1)
+                    grad_conv[start : start + width, :] = piece[:, :width]
+
+
+def replicated_step(gathered, own, weights, w_track_shape, w_conv_shape, table, dilation, rows_total, blocks):
+    strips = gathered.shape[0]
+    layers = w_track_shape[0]
+    margin = rows_total // 4
+    size = rows_total * blocks
+    chan_count = w_track_shape[2]
+    det_count, band_count = table.shape
+    loss_scale = 1.0 / math.sqrt(rows_total * blocks * SLOTS)
+    slots = jnp.eye(SLOTS, dtype=table.dtype)
+    table_t = (slots[:, None, :, None] * table.T[None, :, None, :]).reshape(SLOTS * band_count, SLOTS * det_count)
+    smem = pl.BlockSpec(memory_space=pltpu.SMEM)
+    vmem = pl.BlockSpec(memory_space=pltpu.VMEM)
+    f32, bf16 = jnp.float32, jnp.bfloat16
+    taps = math.prod(w_conv_shape[:4])
+    outs = pl.pallas_call(
+        lambda *refs: step_kernel(rows_total, blocks, margin, loss_scale, *refs),
+        out_shape=(
+            jax.ShapeDtypeStruct((rows_total, LANES), bf16),
+            jax.ShapeDtypeStruct((band_count, chan_count), f32),
+            jax.ShapeDtypeStruct((taps, w_conv_shape[4]), f32),
+            jax.ShapeDtypeStruct((layers * 3 * chan_count, chan_count), f32),
+            jax.ShapeDtypeStruct((band_count, chan_count), f32),
+            jax.ShapeDtypeStruct((band_count, det_count), f32),
+        ),
+        in_specs=[smem, smem] + [vmem] * 8,
+        out_specs=tuple([vmem] * 6),
+        scratch_shapes=[
+            pltpu.VMEM((size, LANES), bf16),
+            pltpu.VMEM((size, LANES), f32),
+            pltpu.VMEM((blocks, LANES), f32),
+            pltpu.VMEM((size + 2 * blocks, 6 * LANES), bf16),
+            pltpu.VMEM((size + 2 * blocks, 6 * LANES), bf16),
+            pltpu.VMEM((layers + 1, size + 2 * margin * blocks, 4 * LANES), bf16),
+            pltpu.VMEM((size + 2 * margin * blocks, 4 * LANES), bf16),
+            pltpu.VMEM((layers + 1, size, 4 * LANES), f32),
+            pltpu.VMEM((size, 4 * LANES), f32),
+            pltpu.VMEM((size, LANES), f32),
+        ],
+        interpret=INTERPRET,
+        name="strip_step",
+    )(own, dilation, gathered, *weights, table_t)
+    prediction, grad_in, grad_conv, grad_track, grad_out_t, grad_table_t = outs
+    return (
+        prediction,
+        grad_in,
+        grad_conv.reshape(w_conv_shape),
+        grad_track.reshape(w_track_shape),
+        grad_out_t.T,
+        grad_table_t.T,
+    )
+
+
+def device_payload(bands, target, detector, flags, blocks):
+    cells = jnp.concatenate([detector & 255, detector >> 8, flags]).astype(jnp.bfloat16)
+    line = jnp.zeros((16, LANES), jnp.bfloat16).at[0, : cells.shape[0]].set(cells)
+    return jnp.concatenate([bands.reshape(bands.shape[0] * blocks, LANES), target, line], axis=0)
+
+
+def gather_strip(payload, size):
+    held = payload[None]
+    distance = size // 2
+    while distance:
+        pairs = [(i, i ^ distance) for i in range(size)]
+        held = jnp.concatenate([held, lax.ppermute(held, "strip", pairs)], axis=0)
+        distance //= 2
+    return held
+
+
+def body_replicated(bands, target, w_in, w_conv, w_track, w_out, table, dilation, detector, flags):
+    size = lax.axis_size("strip")
+    rows_total = bands.shape[0] * size
+    blocks = bands.shape[1] // LANES
+    own = lax.axis_index("strip").astype(jnp.int32).reshape(1)
+    weights = prepare_weights(w_in, w_conv, w_track, w_out)
+    gathered = gather_strip(device_payload(bands, target, detector, flags, blocks), size)
+    return replicated_step(
+        gathered, own, weights, w_track.shape, w_conv.shape, table, dilation, rows_total, blocks
+    )
+
+
+def strip_fits(bands, target, w_in, w_conv, w_track, w_out, table, dilation, detector, flags):
+    size = lax.axis_size("strip")
+    band_count, chan_count = w_in.shape
+    rows_local = bands.shape[0]
+    rows_total = rows_local * size
+    blocks = bands.shape[1] // LANES
+    held = rows_total * blocks * SLOTS * chan_count * 44
+    return (
+        size & (size - 1) == 0
+        and chan_count == 2 * HALF
+        and band_count * SLOTS == LANES
+        and w_conv.shape[2:] == (4, HALF // 2, HALF // 2)
+        and w_out.shape[1] == band_count
+        and target.shape == (rows_total, LANES)
+        and blocks == size
+        and blocks % 16 == 0
+        and held <= VMEM_BUDGET
+    )
+
+
+def body(*args):
+    return body_replicated(*args) if strip_fits(*args) else body_distributed(*args)
+
+
 def solution(mesh):
     placed = (
         P(("groups", "strip"), None),

time: 163 us -> 40.8 us (0.25)
  blocking collectives: 59.5 us -> 0 us
  waiting for transfers between devices: 36.8 us -> 5.23 us
  between operations: 20.5 us -> 0.7 us
  Pallas kernels: 0 us -> 18.5 us
  starting transfers between devices: 22.6 us -> 7.59 us
  matrix products: 10.5 us -> 0 us
  local copies, waits for them, and re-layouts: 9.7 us -> 5.37 us
    psum x1 -> x0, blocking collectives: 59.5 us -> none  [body(): lax.psum((grad_in, grad_conv, grad_track, grad_out, grad_table), 'strip')]
    psum x1 -> x0, waiting for transfers between devices: 32.3 us -> none  [body(): lax.psum((grad_in, grad_conv, grad_track, grad_out, grad_table), 'strip')]
    pallas_call x0 -> x2, Pallas kernels: none -> 18.5 us  [the longest x1 14.9 us: replicated_step(): pl.pallas_call(lambda *refs: step_kernel(rows_total, blocks, margin, loss...]
    all_to_all x2 -> x0, starting transfers between devices: 13.9 us -> none  [the longest x1 7.95 us: body(): lax.all_to_all(features, 'strip', split_axis=1, concat_axis=0, tiled=True)]
    dot_general x60 -> x0, matrix products: 10.5 us -> none  [the longest x9 1.67 us: conv_weight_grad(): lax.dot_general(window, flat_out, contract, preferred_element_type=jnp.fl...]
    ppermute x4, waiting for transfers between devices: 0.02 us -> 5.23 us  [gather_strip(): held = jnp.concatenate([held, lax.ppermute(held, 'strip', pairs)], axis=0)]
    all_to_all x2 -> x0, waiting for transfers between devices: 4.55 us -> none  [the longest x1 4.5 us: body(): lax.all_to_all(feature_grad, 'strip', split_axis=0, concat_axis=1, tiled=...]
    unnamed x16 -> x7, local copies, waits for them, and re-layouts: 2.83 us -> 0.79 us
  transfers between devices with their start and end apart: 7 -> 4, of which waited for: 2 -> 3; matrix products, arithmetic and copies ran while one was open for 6% -> 13% of each run, Pallas kernels for 0% -> 9%
where the time goes in v1:
time: 40.8 us; the launch traced here: 40.4 us
  Pallas kernels  18.5 us (45%)
  starting transfers between devices  7.59 us (19%)
  local copies, waits for them, and re-layouts  5.37 us (13%)
  waiting for transfers between devices  5.23 us (13%)
  other arithmetic  3.01 us (7%)
  between operations  0.7 us (2%)
    pallas_call x1, Pallas kernels, replicated_step(): pl.pallas_call(lambda *refs: step_kernel(rows_total, blocks, margin, loss...  14.9 us
    ppermute x4, starting transfers between devices, gather_strip(): held = jnp.concatenate([held, lax.ppermute(held, 'strip', pairs)], axis=0)  7.59 us
    ppermute x4, waiting for transfers between devices, gather_strip(): held = jnp.concatenate([held, lax.ppermute(held, 'strip', pairs)], axis=0)  5.23 us
    pallas_call x1, Pallas kernels, prepare_weights(): pl.pallas_call(prepare_kernel, out_shape=tuple((jax.ShapeDtypeStruct(s, j...  3.58 us
    transpose x1, local copies, waits for them, and re-layouts, prepare_weights(): taps = jnp.transpose(w_conv, (0, 1, 3, 2, 4)).reshape(9 * width, chan_count)  1.11 us
    mul x1, local copies, waits for them, and re-layouts, replicated_step(): slots[:, None, :, None] * table.T[None, :, None, :]  0.85 us
    reshape x1, local copies, waits for them, and re-layouts, prepare_weights(): jnp.transpose(w_conv, (0, 1, 4, 2, 3)).reshape(9 * width, chan_count)  0.82 us
    mul x1, other arithmetic, replicated_step(): slots[:, None, :, None] * table.T[None, :, None, :]  0.82 us
  transfers between devices with their start and end apart: 4, of which 3 were waited for; matrix products, arithmetic and copies ran while one was open for 13% of the time, Pallas kernels for 9%

profile of v1, /device:TPU:0, one launch (start us, length us, event | category | flops | bytes accessed | tf_op | source)
XLA Modules:
  0.0 40.4 jit_solution(13233434581701810683)
XLA Ops:
  0.6 0.0 copy-start
  0.6 0.8 %reshape.104 = bf16[32,128]{1,0:T(8,128)(2,1)S(1)} reshape(bf16[2,2048]{1,0:T(2,128)(2,1)} %param.12) | data formatting | bytes 16384 | tf_op jit(solution)/shard_map/reshape | solution.py:640
  1.4 0.7 %convert_bitcast_fusion.2 = (bf16[1,4]{1,0:T(2,128)(2,1)S(1)}, bf16[1,4]{1,0:T(2,128)(2,1)S(1)}, bf16[1,4]{1,0:T(2,128)(2,1)S(1)}) fusion(s32[4]{0:T(128)} %param.20, s32[4]{0:T(128)} %param.21), kind=kLoop, calls=%fused_computation.25 | loop fusion | flops 20 | bytes 56 | tf_op jit(solution)/shard_map/concatenate | solution.py:638
  2.1 0.1 fusion.8
  2.2 0.7 %maximum_bitcast_fusion = bf16[1,80,128]{2,1,0:T(8,128)(2,1)S(1)} fusion(bf16[16,128]{1,0:T(8,128)(2,1)S(1)} %fusion.8, bf16[32,128]{1,0:T(8,128)(2,1)} %param.13, bf16[32,128]{1,0:T(8,128)(2,1)S(1)} %reshape.104), kind=kLoop, calls=%fused_computation.4 | loop fusion | flops 61440 | bytes 40960 | tf_op jit(solution)/shard_map/broadcast_in_dim | solution.py:644
  2.9 4.1 %collective-permute-start = (bf16[1,80,128]{2,1,0:T(8,128)(2,1)S(1)}, bf16[1,80,128]{2,1,0:T(8,128)(2,1)S(1)}, u32[]{:S(2)}, u32[]{:S(2)}) collective-permute-start(bf16[1,80,128]{2,1,0:T(8,128)(2,1)S(1)} %maximum_bitcast_fusion), channel_id=1, source_target_pairs={{0,8},{1,9},{2,10},{3,11},{4,12},{5,13},{6,14},{7,15},{8,0},{9,1},... | collective-permute-start | bytes 61448 | tf_op jit(solution)/shard_map/ppermute | solution.py:648
  6.9 0.8 %broadcast_multiply_fusion = f32[4,32,4,64]{3,2,1,0:T(4,128)S(1)} fusion(f32[32,64]{1,0:T(8,128)} %bitcast.21, f32[4,4]{1,0:T(4,128)S(1)} %fusion.9), kind=kLoop, calls=%fused_computation.1 | loop fusion | flops 32768 | bytes 139328 | tf_op jit(solution)/shard_map/mul | solution.py:594
  7.7 0.9 %collective-permute-done = bf16[1,80,128]{2,1,0:T(8,128)(2,1)S(1)} collective-permute-done((bf16[1,80,128]{2,1,0:T(8,128)(2,1)S(1)}, bf16[1,80,128]{2,1,0:T(8,128)(2,1)S(1)}, u32[]{:S(2)}, u32[]{:S(2)}) %collective-permute-start) | collective-permute-done | bytes 20512 | tf_op jit(solution)/shard_map/ppermute | solution.py:648
  8.7 1.9 %collective-permute-start.1 = (bf16[2,80,128]{2,1,0:T(8,128)(2,1)S(1)}, bf16[2,80,128]{2,1,0:T(8,128)(2,1)S(1)}, u32[]{:S(2)}, u32[]{:S(2)}) collective-permute-start(bf16[2,80,128]{2,1,0:T(8,128)(2,1)S(1)} %pad_maximum_fusion.2), channel_id=1, source_target_pairs={{0,4},{1,5},{2,6},{3,7},{4,0},{5,1},{6,2},{7,3},{8,12},{9,13},{10,... | collective-permute-start | bytes 122888 | tf_op jit(solution)/shard_map/ppermute | solution.py:648
  10.6 0.7 %constant_dynamic-update-slice_fusion.4 = bf16[16,80,128]{2,1,0:T(8,128)(2,1)S(1)} fusion(bf16[16,128]{1,0:T(8,128)(2,1)S(1)} %fusion.8, bf16[32,128]{1,0:T(8,128)(2,1)} %param.13, bf16[32,128]{1,0:T(8,128)(2,1)S(1)} %reshape.104), kind=kLoop, calls=%fused_computation.9 | loop fusion | flops 61439 | bytes 40960
  11.3 0.8 %mul.20.refs_9_ = f32[128,256]{1,0:T(8,128)} reshape(f32[4,32,4,64]{3,2,1,0:T(4,128)S(1)} %broadcast_multiply_fusion) | data formatting | bytes 262144 | tf_op jit(solution)/shard_map/mul | solution.py:594
  12.1 1.1 %copy.16 = bf16[3,3,32,4,32]{4,3,2,1,0:T(4,128)(2,1)S(1)} copy(bf16[3,3,32,4,32]{4,2,3,1,0:T(8,128)(2,1)} %bitcast.19) | data formatting | bytes 147456 | tf_op jit(solution)/shard_map/transpose | solution.py:320
  13.3 0.8 %reshape.105.taps = bf16[288,128]{1,0:T(8,128)(2,1)} reshape(bf16[3,3,32,4,32]{4,3,2,1,0:T(4,128)(2,1)S(1)} %copy.16) | data formatting | bytes 147456 | tf_op jit(solution)/shard_map/reshape | solution.py:320
  14.1 0.0 copy-done
  14.1 0.2 copy.17
  14.3 0.8 %reshape.106.taps_t = bf16[288,128]{1,0:T(8,128)(2,1)} reshape(bf16[3,3,32,4,32]{4,3,2,1,0:T(4,128)(2,1)S(1)} %copy.17) | data formatting | bytes 147456 | tf_op jit(solution)/shard_map/reshape | solution.py:321
  15.1 3.6 %prepare_weights.1 = (bf16[128,512]{1,0:T(8,128)(2,1)}, bf16[128,512]{1,0:T(8,128)(2,1)}, bf16[2,1152,256]{2,1,0:T(8,128)(2,1)}, bf16[2,1152,256]{2,1,0:T(8,128)...) custom-call(bf16[32,128]{1,0:T(8,128)(2,1)} %w_in.1, bf16[32,128]{1,0:T(8,128)(2,1)} %bitcast.22, ...), custom_call_target="tpu_custom_call" | custom-call | tf_op jit(solution)/shard_map/prepare_weights/pallas_call | solution.py:330
  18.7 0.0 collective-permute-done.1
  18.7 1.6 %collective-permute-start.2 = (bf16[4,80,128]{2,1,0:T(8,128)(2,1)S(1)}, bf16[4,80,128]{2,1,0:T(8,128)(2,1)S(1)}, u32[]{:S(2)}, u32[]{:S(2)}) collective-permute-start(bf16[4,80,128]{2,1,0:T(8,128)(2,1)S(1)} %pad_maximum_fusion.1), channel_id=1, source_target_pairs={{0,2},{1,3},{2,0},{3,1},{4,6},{5,7},{6,4},{7,5},{8,10},{9,11},{10,... | collective-permute-start | bytes 245768 | tf_op jit(solution)/shard_map/ppermute | solution.py:648
  20.3 2.9 %collective-permute-done.2 = bf16[4,80,128]{2,1,0:T(8,128)(2,1)S(1)} collective-permute-done((bf16[4,80,128]{2,1,0:T(8,128)(2,1)S(1)}, bf16[4,80,128]{2,1,0:T(8,128)(2,1)S(1)}, u32[]{:S(2)}, u32[]{:S(2)}) %collective-permute-start.2) | collective-permute-done | bytes 81952 | tf_op jit(solution)/shard_map/ppermute | solution.py:648
  23.2 0.1 collective-permute-start.3
  23.4 1.3 %collective-permute-done.3 = bf16[8,80,128]{2,1,0:T(8,128)(2,1)S(1)} collective-permute-done((bf16[8,80,128]{2,1,0:T(8,128)(2,1)S(1)}, bf16[8,80,128]{2,1,0:T(8,128)(2,1)S(1)}, u32[]{:S(2)}, u32[]{:S(2)}) %collective-permute-start.3) | collective-permute-done | bytes 163872 | tf_op jit(solution)/shard_map/ppermute | solution.py:648
  24.7 0.0 copy-start.1
  24.7 0.7 %copy-done.1 = bf16[16,80,128]{2,1,0:T(8,128)(2,1)} copy-done((bf16[16,80,128]{2,1,0:T(8,128)(2,1)}, bf16[16,80,128]{2,1,0:T(8,128)(2,1)S(1)}, u32[]{:S(2)}) %copy-start.1) | copy-done | bytes 327704
  25.5 14.9 %strip_step.1 = (bf16[32,128]{1,0:T(8,128)(2,1)}, f32[32,128]{1,0:T(8,128)}, f32[1152,32]{1,0:T(8,128)}, f32[1152,128]{1,0:T(8,128)}, f32[32,128]{1,0:T(8,128)}, /*index=5*/f32[32,64]{1,0:T(8,128)}) custom-call(s32[1]{0:T(128)} %bitcast.refs_0_, s32[3]{0:T(128)} %refs_1_.1, bf16[16,80,128]{2,1,0:T(8,128)(2,1)} %copy-done.1, ...), custom_call_target="tpu_custom_call" | custom-call | tf_op jit(solution)/shard_map/strip_step/pallas_call | solution.py:599
  (8 shorter events, 0.1 us)
Async XLA Ops:
  0.6 13.4 %copy-start = (bf16[3,3,4,32,32]{4,3,2,1,0:T(8,128)(2,1)S(1)}, bf16[3,3,4,32,32]{4,3,2,1,0:T(8,128)(2,1)}, u32[]{:S(2)}) copy-start(bf16[3,3,4,32,32]{4,3,2,1,0:T(8,128)(2,1)} %param.15) | copy-start | bytes 221188
  2.9 5.8 %collective-permute-start = (bf16[1,80,128]{2,1,0:T(8,128)(2,1)S(1)}, bf16[1,80,128]{2,1,0:T(8,128)(2,1)S(1)}, u32[]{:S(2)}, u32[]{:S(2)}) collective-permute-start(bf16[1,80,128]{2,1,0:T(8,128)(2,1)S(1)} %maximum_bitcast_fusion), channel_id=1, source_target_pairs={{0,8},{1,9},{2,10},{3,11},{4,12},{5,13},{6,14},{7,15},{8,0},{9,1},... | collective-permute-start | bytes 61448 | tf_op jit(solution)/shard_map/ppermute | solution.py:648
  8.7 10.0 %collective-permute-start.1 = (bf16[2,80,128]{2,1,0:T(8,128)(2,1)S(1)}, bf16[2,80,128]{2,1,0:T(8,128)(2,1)S(1)}, u32[]{:S(2)}, u32[]{:S(2)}) collective-permute-start(bf16[2,80,128]{2,1,0:T(8,128)(2,1)S(1)} %pad_maximum_fusion.2), channel_id=1, source_target_pairs={{0,4},{1,5},{2,6},{3,7},{4,0},{5,1},{6,2},{7,3},{8,12},{9,13},{10,... | collective-permute-start | bytes 122888 | tf_op jit(solution)/shard_map/ppermute | solution.py:648
  18.7 4.5 %collective-permute-start.2 = (bf16[4,80,128]{2,1,0:T(8,128)(2,1)S(1)}, bf16[4,80,128]{2,1,0:T(8,128)(2,1)S(1)}, u32[]{:S(2)}, u32[]{:S(2)}) collective-permute-start(bf16[4,80,128]{2,1,0:T(8,128)(2,1)S(1)} %pad_maximum_fusion.1), channel_id=1, source_target_pairs={{0,2},{1,3},{2,0},{3,1},{4,6},{5,7},{6,4},{7,5},{8,10},{9,11},{10,... | collective-permute-start | bytes 245768 | tf_op jit(solution)/shard_map/ppermute | solution.py:648
  23.2 1.5 %collective-permute-start.3 = (bf16[8,80,128]{2,1,0:T(8,128)(2,1)S(1)}, bf16[8,80,128]{2,1,0:T(8,128)(2,1)S(1)}, u32[]{:S(2)}, u32[]{:S(2)}) collective-permute-start(bf16[8,80,128]{2,1,0:T(8,128)(2,1)S(1)} %pad_maximum_fusion), channel_id=1, source_target_pairs={{0,1},{1,0},{2,3},{3,2},{4,5},{5,4},{6,7},{7,6},{8,9},{9,8},{10,11... | collective-permute-start | bytes 491528 | tf_op jit(solution)/shard_map/ppermute | solution.py:648
  24.7 0.8 %copy-start.1 = (bf16[16,80,128]{2,1,0:T(8,128)(2,1)}, bf16[16,80,128]{2,1,0:T(8,128)(2,1)S(1)}, u32[]{:S(2)}) copy-start(bf16[16,80,128]{2,1,0:T(8,128)(2,1)S(1)} %constant_dynamic-update-slice_fusion.refs_2_) | copy-start | bytes 983044

commit v2 on v1

--- a/solution.py
+++ b/solution.py
@@ -228,6 +228,8 @@
 HALF = 64
 SLOTS = 4
 VMEM_BUDGET = 48 * 1024 * 1024
+PREPARE_VMEM = 16 * 1024 * 1024
+STEP_VMEM = 32 * 1024 * 1024
 
 
 def low_half(shape):
@@ -271,7 +273,7 @@
 
 
 def expand_conv(taps, ref, transposed):
-    width = taps.shape[0] // 9
+    width = taps[0].shape[0]
     low = low_half((HALF, LANES))
     zero = jnp.zeros((HALF, LANES), jnp.float32)
     row = lax.broadcasted_iota(jnp.int32, (HALF, LANES), 0) // width
@@ -281,7 +283,7 @@
         for h in range(2):
             values = []
             for j in range(3):
-                tap = taps[(3 * i + j) * width : (3 * i + j + 1) * width]
+                tap = taps[3 * i + j]
                 turned = swap_halves(tap)
                 spread = jnp.where(low[:width], tap, turned) if h == 0 else jnp.where(low[:width], turned, tap)
                 values.append(jnp.where(same, jnp.concatenate([spread, spread], axis=0), zero))
@@ -299,26 +301,55 @@
                 ref[h, start : start + HALF, :] = jnp.concatenate(tiles, axis=1).astype(ref.dtype)
 
 
-def prepare_kernel(w_in, w_out_t, taps, taps_t, w_track, w4, wo4, wc, wt, wf, wb):
-    w4[...] = expand_band(w_in[...].astype(jnp.float32)).astype(w4.dtype)
-    wo4[...] = expand_band(w_out_t[...].astype(jnp.float32)).astype(wo4.dtype)
-    expand_conv(taps[...].astype(jnp.float32), wc, False)
-    expand_conv(taps_t[...].astype(jnp.float32), wt, True)
-    layers = w_track.shape[0]
-    for layer in range(layers):
+def stay(x):
+    return x if INTERPRET else pltpu.with_memory_space_constraint(x, pltpu.HBM)
+
+
+def fetch(sources, targets, semaphores):
+    copies = [pltpu.make_async_copy(a, b, semaphores.at[n]) for n, (a, b) in enumerate(zip(sources, targets))]
+    for copy in copies:
+        copy.start()
+    return copies
+
+
+def prepare_kernel(*refs):
+    sources, (w4, wo4, wc, wt, wf, wb, tt), held, semaphores = refs[:5], refs[5:12], refs[12:17], refs[17]
+    w_track, w_conv, w_in, w_out_t, table_t = held
+    copies = fetch(sources, held, semaphores)
+    for copy in copies:
+        copy.wait()
+    f32 = jnp.float32
+    w4[...] = expand_band(w_in[...].astype(f32)).astype(w4.dtype)
+    wo4[...] = expand_band(w_out_t[...].astype(f32)).astype(wo4.dtype)
+    width = w_conv.shape[1]
+    groups = LANES // width
+    taps, taps_t = [], []
+    for tap in range(9):
+        block = w_conv[tap * LANES : (tap + 1) * LANES, :].astype(f32)
+        taps.append(jnp.concatenate([block[g * width : (g + 1) * width] for g in range(groups)], axis=1))
+        taps_t.append(block.T)
+    expand_conv(taps, wc, False)
+    expand_conv(taps_t, wt, True)
+    for layer in range(w_track.shape[0]):
         for tap in range(3):
-            weight = w_track[layer, tap].astype(jnp.float32)
+            weight = w_track[layer, tap].astype(f32)
             rows = pl.ds(tap * 2 * LANES, 2 * LANES)
             wf[layer, rows, :] = expand_tap(weight).astype(wf.dtype)
             wb[layer, rows, :] = expand_tap(weight.T).astype(wb.dtype)
-
-
-def prepare_weights(w_in, w_conv, w_track, w_out):
+    rows, columns = table_t.shape
+    for place, part in enumerate(thirds(table_t[...])):
+        part = part.astype(f32)
+        zero = jnp.zeros_like(part)
+        for k in range(SLOTS):
+            line = jnp.concatenate([part if k == other else zero for other in range(SLOTS)], axis=1)
+            tt[k * rows : (k + 1) * rows, place * SLOTS * columns : (place + 1) * SLOTS * columns] = line.astype(tt.dtype)
+
+
+def prepare_weights(w_in, w_conv, w_track, w_out, table):
     chan_count = w_in.shape[1]
-    width = w_conv.shape[3]
+    width = w_conv.shape[4]
     layers = w_track.shape[0]
-    taps = jnp.transpose(w_conv, (0, 1, 3, 2, 4)).reshape(9 * width, chan_count)
-    taps_t = jnp.transpose(w_conv, (0, 1, 4, 2, 3)).reshape(9 * width, chan_count)
+    sources = (w_track, w_conv.reshape(-1, width), w_in, w_out.T, table.T)
     shapes = (
         (SLOTS * w_in.shape[0], SLOTS * chan_count),
         (SLOTS * w_out.shape[1], SLOTS * chan_count),
@@ -326,13 +357,17 @@
         (2, 18 * HALF, 2 * LANES),
         (layers, 6 * LANES, 2 * LANES),
         (layers, 6 * LANES, 2 * LANES),
+        (SLOTS * table.shape[1], 3 * SLOTS * table.shape[0]),
     )
     return pl.pallas_call(
         prepare_kernel,
         out_shape=tuple(jax.ShapeDtypeStruct(s, jnp.bfloat16) for s in shapes),
+        in_specs=[pl.BlockSpec(memory_space=pltpu.HBM)] * len(sources),
+        scratch_shapes=[pltpu.VMEM(a.shape, a.dtype) for a in sources] + [pltpu.SemaphoreType.DMA((len(sources),))],
+        compiler_params=pltpu.CompilerParams(vmem_limit_bytes=PREPARE_VMEM),
         interpret=INTERPRET,
         name="prepare_weights",
-    )(w_in, w_out.T, taps, taps_t, w_track)
+    )(*[stay(a) for a in sources])
 
 
 def silu_and_slope(v):
@@ -424,7 +459,7 @@
             place = place * 2 + ((apart >> b) & 1)
         pixels[s * local : (s + 1) * local, :] = gathered[place, 0:local, :]
         target[pl.ds(s, rows_total, stride=blocks), :] = gathered[place, local : local + rows_total, :].astype(f32)
-        meta[s : s + 1, :] = gathered[place, local + rows_total : local + rows_total + 16, :].astype(f32)[0:1]
+        meta[s : s + 1, :] = gathered[place, local + rows_total : local + rows_total + 8, :].astype(f32)[0:1]
 
     for ref in (proj, mixed):
         ref[0:blocks, :] = jnp.zeros((blocks, ref.shape[1]), bf16)
@@ -486,7 +521,7 @@
 
     lax.fori_loop(0, layers, forward, 0)
 
-    det_count = table_t.shape[1] // SLOTS
+    det_count = table_t.shape[1] // (3 * SLOTS)
     meta_b = meta[...].astype(bf16)
     source = lax.broadcasted_iota(jnp.int32, (LANES, SLOTS * det_count), 0)
     slot_of = lax.broadcasted_iota(jnp.int32, (LANES, SLOTS * det_count), 1) // det_count
@@ -496,7 +531,7 @@
     source = lax.broadcasted_iota(jnp.int32, (LANES, LANES), 0)
     slot_of = lax.broadcasted_iota(jnp.int32, (LANES, LANES), 1) // (LANES // SLOTS)
     flag = dot(meta_b, jnp.where(source == slot_of + 2 * SLOTS, 1.0, 0.0).astype(bf16))
-    offsets = sum(dot_nt(selector, part) for part in thirds(table_t[...])) * flag
+    offsets = dot_nt(jnp.concatenate([selector] * 3, axis=1), table_t[...]) * flag
 
     raw = dot_nt(acts[layers, middle, :], wo4[...]).reshape(rows_total, blocks, LANES) + offsets[None]
     rounded = raw.astype(bf16).astype(f32)
@@ -582,16 +617,14 @@
                     grad_conv[start : start + width, :] = piece[:, :width]
 
 
-def replicated_step(gathered, own, weights, w_track_shape, w_conv_shape, table, dilation, rows_total, blocks):
+def replicated_step(gathered, own, weights, w_track_shape, w_conv_shape, table_shape, dilation, rows_total, blocks):
     strips = gathered.shape[0]
     layers = w_track_shape[0]
     margin = rows_total // 4
     size = rows_total * blocks
     chan_count = w_track_shape[2]
-    det_count, band_count = table.shape
+    det_count, band_count = table_shape
     loss_scale = 1.0 / math.sqrt(rows_total * blocks * SLOTS)
-    slots = jnp.eye(SLOTS, dtype=table.dtype)
-    table_t = (slots[:, None, :, None] * table.T[None, :, None, :]).reshape(SLOTS * band_count, SLOTS * det_count)
     smem = pl.BlockSpec(memory_space=pltpu.SMEM)
     vmem = pl.BlockSpec(memory_space=pltpu.VMEM)
     f32, bf16 = jnp.float32, jnp.bfloat16
@@ -620,9 +653,10 @@
             pltpu.VMEM((size, 4 * LANES), f32),
             pltpu.VMEM((size, LANES), f32),
         ],
+        compiler_params=pltpu.CompilerParams(vmem_limit_bytes=STEP_VMEM),
         interpret=INTERPRET,
         name="strip_step",
-    )(own, dilation, gathered, *weights, table_t)
+    )(own, dilation, gathered, *weights)
     prediction, grad_in, grad_conv, grad_track, grad_out_t, grad_table_t = outs
     return (
         prediction,
@@ -634,10 +668,48 @@
     )
 
 
+def payload_kernel(*refs):
+    sources, payload, held, rows, semaphores = refs[:4], refs[4], refs[5:9], refs[9], refs[10]
+    bands, target, detector, flags = held
+    for copy in fetch(sources, held, semaphores):
+        copy.wait()
+    blocks = bands.shape[1] // LANES
+    rows_local = bands.shape[0]
+    local = rows_local * blocks
+    wide = bands[...].astype(jnp.float32)
+    for block in range(blocks):
+        rows[pl.ds(block, rows_local, stride=blocks), :] = wide[:, block * LANES : (block + 1) * LANES]
+    payload[0:local, :] = rows[...].astype(payload.dtype)
+    payload[local : local + target.shape[0], :] = target[...]
+    shape = (8, LANES)
+    lane = lax.broadcasted_iota(jnp.int32, shape, 1)
+    line = jnp.zeros(shape, jnp.int32)
+    for k in range(SLOTS):
+        line = jnp.where(lane == k, detector[k] & 255, line)
+        line = jnp.where(lane == SLOTS + k, detector[k] >> 8, line)
+        line = jnp.where(lane == 2 * SLOTS + k, flags[k], line)
+    payload[local + target.shape[0] :, :] = line.astype(jnp.float32).astype(payload.dtype)
+
+
 def device_payload(bands, target, detector, flags, blocks):
-    cells = jnp.concatenate([detector & 255, detector >> 8, flags]).astype(jnp.bfloat16)
-    line = jnp.zeros((16, LANES), jnp.bfloat16).at[0, : cells.shape[0]].set(cells)
-    return jnp.concatenate([bands.reshape(bands.shape[0] * blocks, LANES), target, line], axis=0)
+    local = bands.shape[0] * blocks
+    return pl.pallas_call(
+        payload_kernel,
+        out_shape=jax.ShapeDtypeStruct((local + target.shape[0] + 8, LANES), jnp.bfloat16),
+        in_specs=[pl.BlockSpec(memory_space=pltpu.HBM)] * 4,
+        out_specs=pl.BlockSpec(memory_space=pltpu.VMEM),
+        scratch_shapes=[
+            pltpu.VMEM(bands.shape, bands.dtype),
+            pltpu.VMEM(target.shape, target.dtype),
+            pltpu.SMEM(detector.shape, detector.dtype),
+            pltpu.SMEM(flags.shape, flags.dtype),
+            pltpu.VMEM((local, LANES), jnp.float32),
+            pltpu.SemaphoreType.DMA((4,)),
+        ],
+        compiler_params=pltpu.CompilerParams(vmem_limit_bytes=PREPARE_VMEM),
+        interpret=INTERPRET,
+        name="payload",
+    )(*[stay(a) for a in (bands, target, detector, flags)])
 
 
 def gather_strip(payload, size):
@@ -655,10 +727,10 @@
     rows_total = bands.shape[0] * size
     blocks = bands.shape[1] // LANES
     own = lax.axis_index("strip").astype(jnp.int32).reshape(1)
-    weights = prepare_weights(w_in, w_conv, w_track, w_out)
+    weights = prepare_weights(w_in, w_conv, w_track, w_out, table)
     gathered = gather_strip(device_payload(bands, target, detector, flags, blocks), size)
     return replicated_step(
-        gathered, own, weights, w_track.shape, w_conv.shape, table, dilation, rows_total, blocks
+        gathered, own, weights, w_track.shape, w_conv.shape, table.shape, dilation, rows_total, blocks
     )
 
 

time: 40.8 us -> 30.3 us (0.74)
  local copies, waits for them, and re-layouts: 5.37 us -> 0.06 us
  other arithmetic: 3.01 us -> 0.03 us
  Pallas kernels: 18.5 us -> 15.7 us
  starting transfers between devices: 7.59 us -> 8.07 us
    reshape x3 -> x0, local copies, waits for them, and re-layouts: 2.39 us -> none  [the longest x1 0.82 us: prepare_weights(): jnp.transpose(w_conv, (0, 1, 4, 2, 3)).reshape(9 * width, chan_count)]
    pallas_call x1, Pallas kernels: 14.9 us -> 12.8 us  [replicated_step(): pl.pallas_call(lambda *refs: step_kernel(rows_total, blocks, margin, loss...]
    pallas_call x1, Pallas kernels: 3.58 us -> 1.97 us  [prepare_weights(): pl.pallas_call(prepare_kernel, out_shape=tuple((jax.ShapeDtypeStruct(s, j...]
    transpose x2 -> x0, local copies, waits for them, and re-layouts: 1.32 us -> none  [the longest x1 1.11 us: prepare_weights(): taps = jnp.transpose(w_conv, (0, 1, 3, 2, 4)).reshape(9 * width, chan_count)]
    pallas_call x0 -> x1, Pallas kernels: none -> 0.86 us  [device_payload(): pl.pallas_call(payload_kernel, out_shape=jax.ShapeDtypeStruct((local + ta...]
    mul x1 -> x0, local copies, waits for them, and re-layouts: 0.85 us -> none  [replicated_step(): slots[:, None, :, None] * table.T[None, :, None, :]]
    mul x1 -> x0, other arithmetic: 0.82 us -> none  [replicated_step(): slots[:, None, :, None] * table.T[None, :, None, :]]
    concatenate x2 -> x0, other arithmetic: 0.75 us -> none  [device_payload(): jnp.concatenate([detector & 255, detector >> 8, flags]).astype(jnp.bfloat16)]
  transfers between devices with their start and end apart: 4 -> 4, of which waited for: 3 -> 4; matrix products, arithmetic and copies ran while one was open for 13% -> 0% of each run, Pallas kernels for 9% -> 7%
where the time goes in v2:
time: 30.3 us; the launch traced here: 30.1 us
  Pallas kernels  15.7 us (52%)
  starting transfers between devices  8.07 us (27%)
  waiting for transfers between devices  5.58 us (18%)
  between operations  0.7 us (2%)
    pallas_call x1, Pallas kernels, replicated_step(): pl.pallas_call(lambda *refs: step_kernel(rows_total, blocks, margin, loss...  12.8 us
    ppermute x4, starting transfers between devices, gather_strip(): held = jnp.concatenate([held, lax.ppermute(held, 'strip', pairs)], axis=0)  8.07 us
    ppermute x4, waiting for transfers between devices, gather_strip(): held = jnp.concatenate([held, lax.ppermute(held, 'strip', pairs)], axis=0)  5.58 us
    pallas_call x1, Pallas kernels, prepare_weights(): pl.pallas_call(prepare_kernel, out_shape=tuple((jax.ShapeDtypeStruct(s, j...  1.97 us
    pallas_call x1, Pallas kernels, device_payload(): pl.pallas_call(payload_kernel, out_shape=jax.ShapeDtypeStruct((local + ta...  0.86 us
  transfers between devices with their start and end apart: 4, of which 4 were waited for; matrix products, arithmetic and copies ran while one was open for 0% of the time, Pallas kernels for 7%

profile of v2, /device:TPU:0, one launch (start us, length us, event | category | flops | bytes accessed | tf_op | source)
XLA Modules:
  0.0 30.1 jit_solution(1172129664981720686)
XLA Ops:
  0.6 0.0 copy-start
  0.6 0.9 %payload.1 = bf16[72,128]{1,0:T(8,128)(2,1)S(1)} custom-call(bf16[2,2048]{1,0:T(2,128)(2,1)} %refs_0_.2, bf16[32,128]{1,0:T(8,128)(2,1)} %refs_1_.2, s32[4]{0:T(128)} %refs_2_.2, s32[4]{0:T(128)} %refs_3_.1), custom_call_target="tpu_custom_call" | custom-call | tf_op jit(solution)/shard_map/payload/pallas_call | solution.py:696
  1.5 4.1 %collective-permute-start = (bf16[1,72,128]{2,1,0:T(8,128)(2,1)S(1)}, bf16[1,72,128]{2,1,0:T(8,128)(2,1)S(1)}, u32[]{:S(2)}, u32[]{:S(2)}) collective-permute-start(bf16[1,72,128]{2,1,0:T(8,128)(2,1)S(1)} %bitcast.10), channel_id=1, source_target_pairs={{0,8},{1,9},{2,10},{3,11},{4,12},{5,13},{6,14},{7,15},{8,0},{9,1},... | collective-permute-start | bytes 55304 | tf_op jit(solution)/shard_map/ppermute | solution.py:720
  5.6 1.7 %collective-permute-done = bf16[1,72,128]{2,1,0:T(8,128)(2,1)S(1)} collective-permute-done((bf16[1,72,128]{2,1,0:T(8,128)(2,1)S(1)}, bf16[1,72,128]{2,1,0:T(8,128)(2,1)S(1)}, u32[]{:S(2)}, u32[]{:S(2)}) %collective-permute-start) | collective-permute-done | bytes 18464 | tf_op jit(solution)/shard_map/ppermute | solution.py:720
  7.4 1.9 %collective-permute-start.1 = (bf16[2,72,128]{2,1,0:T(8,128)(2,1)S(1)}, bf16[2,72,128]{2,1,0:T(8,128)(2,1)S(1)}, u32[]{:S(2)}, u32[]{:S(2)}) collective-permute-start(bf16[2,72,128]{2,1,0:T(8,128)(2,1)S(1)} %pad_maximum_fusion.2), channel_id=1, source_target_pairs={{0,4},{1,5},{2,6},{3,7},{4,0},{5,1},{6,2},{7,3},{8,12},{9,13},{10,... | collective-permute-start | bytes 110600 | tf_op jit(solution)/shard_map/ppermute | solution.py:720
  9.3 2.0 %prepare_weights.1 = (bf16[128,512]{1,0:T(8,128)(2,1)S(1)}, bf16[128,512]{1,0:T(8,128)(2,1)S(1)}, bf16[2,1152,256]{2,1,0:T(8,128)(2,1)S(1)}, bf16[2,1152,256]{2,...) custom-call(bf16[3,3,128,128]{3,2,1,0:T(8,128)(2,1)} %refs_0_.3, ...), custom_call_target="tpu_custom_call" | custom-call | tf_op jit(solution)/shard_map/prepare_weights/pallas_call | solution.py:362
  11.3 0.1 collective-permute-done.1
  11.4 2.0 %collective-permute-start.2 = (bf16[4,72,128]{2,1,0:T(8,128)(2,1)S(1)}, bf16[4,72,128]{2,1,0:T(8,128)(2,1)S(1)}, u32[]{:S(2)}, u32[]{:S(2)}) collective-permute-start(bf16[4,72,128]{2,1,0:T(8,128)(2,1)S(1)} %pad_maximum_fusion.1), channel_id=1, source_target_pairs={{0,2},{1,3},{2,0},{3,1},{4,6},{5,7},{6,4},{7,5},{8,10},{9,11},{10,... | collective-permute-start | bytes 221192 | tf_op jit(solution)/shard_map/ppermute | solution.py:720
  13.3 2.4 %collective-permute-done.2 = bf16[4,72,128]{2,1,0:T(8,128)(2,1)S(1)} collective-permute-done((bf16[4,72,128]{2,1,0:T(8,128)(2,1)S(1)}, bf16[4,72,128]{2,1,0:T(8,128)(2,1)S(1)}, u32[]{:S(2)}, u32[]{:S(2)}) %collective-permute-start.2) | collective-permute-done | bytes 73760 | tf_op jit(solution)/shard_map/ppermute | solution.py:720
  15.8 0.1 collective-permute-start.3
  15.9 1.3 %collective-permute-done.3 = bf16[8,72,128]{2,1,0:T(8,128)(2,1)S(1)} collective-permute-done((bf16[8,72,128]{2,1,0:T(8,128)(2,1)S(1)}, bf16[8,72,128]{2,1,0:T(8,128)(2,1)S(1)}, u32[]{:S(2)}, u32[]{:S(2)}) %collective-permute-start.3) | collective-permute-done | bytes 147488 | tf_op jit(solution)/shard_map/ppermute | solution.py:720
  17.3 0.0 copy-done
  17.3 12.8 %strip_step.1 = (bf16[32,128]{1,0:T(8,128)(2,1)}, f32[32,128]{1,0:T(8,128)}, f32[1152,32]{1,0:T(8,128)}, f32[1152,128]{1,0:T(8,128)}, f32[32,128]{1,0:T(8,128)}, /*index=5*/f32[32,64]{1,0:T(8,128)}) custom-call(s32[1]{0:T(128)} %bitcast.refs_0_, s32[3]{0:T(128)S(1)} %copy-done, bf16[16,72,128]{2,1,0:T(8,128)(2,1)S(1)} %constant_dynamic-update-slice_fusion.refs_2_, ...), custom_call_target="tpu_custom_call" | custom-call | tf_op jit(solution)/shard_map/strip_step/pallas_call | solution.py:632
  (8 shorter events, 0.1 us)
Async XLA Ops:
  0.6 16.6 %copy-start = (s32[3]{0:T(128)S(1)}, s32[3]{0:T(128)}, u32[]{:S(2)}) copy-start(s32[3]{0:T(128)} %refs_1_.3) | copy-start | bytes 40
  1.5 5.9 %collective-permute-start = (bf16[1,72,128]{2,1,0:T(8,128)(2,1)S(1)}, bf16[1,72,128]{2,1,0:T(8,128)(2,1)S(1)}, u32[]{:S(2)}, u32[]{:S(2)}) collective-permute-start(bf16[1,72,128]{2,1,0:T(8,128)(2,1)S(1)} %bitcast.10), channel_id=1, source_target_pairs={{0,8},{1,9},{2,10},{3,11},{4,12},{5,13},{6,14},{7,15},{8,0},{9,1},... | collective-permute-start | bytes 55304 | tf_op jit(solution)/shard_map/ppermute | solution.py:720
  7.4 4.0 %collective-permute-start.1 = (bf16[2,72,128]{2,1,0:T(8,128)(2,1)S(1)}, bf16[2,72,128]{2,1,0:T(8,128)(2,1)S(1)}, u32[]{:S(2)}, u32[]{:S(2)}) collective-permute-start(bf16[2,72,128]{2,1,0:T(8,128)(2,1)S(1)} %pad_maximum_fusion.2), channel_id=1, source_target_pairs={{0,4},{1,5},{2,6},{3,7},{4,0},{5,1},{6,2},{7,3},{8,12},{9,13},{10,... | collective-permute-start | bytes 110600 | tf_op jit(solution)/shard_map/ppermute | solution.py:720
  11.4 4.4 %collective-permute-start.2 = (bf16[4,72,128]{2,1,0:T(8,128)(2,1)S(1)}, bf16[4,72,128]{2,1,0:T(8,128)(2,1)S(1)}, u32[]{:S(2)}, u32[]{:S(2)}) collective-permute-start(bf16[4,72,128]{2,1,0:T(8,128)(2,1)S(1)} %pad_maximum_fusion.1), channel_id=1, source_target_pairs={{0,2},{1,3},{2,0},{3,1},{4,6},{5,7},{6,4},{7,5},{8,10},{9,11},{10,... | collective-permute-start | bytes 221192 | tf_op jit(solution)/shard_map/ppermute | solution.py:720
  15.8 1.4 %collective-permute-start.3 = (bf16[8,72,128]{2,1,0:T(8,128)(2,1)S(1)}, bf16[8,72,128]{2,1,0:T(8,128)(2,1)S(1)}, u32[]{:S(2)}, u32[]{:S(2)}) collective-permute-start(bf16[8,72,128]{2,1,0:T(8,128)(2,1)S(1)} %pad_maximum_fusion), channel_id=1, source_target_pairs={{0,1},{1,0},{2,3},{3,2},{4,5},{5,4},{6,7},{7,6},{8,9},{9,8},{10,11... | collective-permute-start | bytes 442376 | tf_op jit(solution)/shard_map/ppermute | solution.py:720

commit v3 on v2

--- a/solution.py
+++ b/solution.py
@@ -259,9 +259,9 @@
     low = low_half((band_count, LANES))
     zero = jnp.zeros((band_count, LANES), jnp.float32)
     columns = []
-    for h in range(2):
-        first, second = (weight, turned) if h == 0 else (turned, weight)
-        for pair in range(2):
+    for pair in range(2):
+        for h in range(2):
+            first, second = (weight, turned) if h == 0 else (turned, weight)
             rows = [zero] * SLOTS
             rows[2 * pair] = jnp.where(low, first, zero)
             rows[2 * pair + 1] = jnp.where(low, zero, second)
@@ -298,7 +298,7 @@
                         pieces.append(values[j] if 0 <= j <= 2 else zero)
                     tiles.append(jnp.where(low, pieces[0], pieces[1]))
                 start = (place * len(INPUT_SLOTS) + position) * HALF
-                ref[h, start : start + HALF, :] = jnp.concatenate(tiles, axis=1).astype(ref.dtype)
+                ref[h, start : start + HALF, :] = (0.5 * jnp.concatenate(tiles, axis=1)).astype(ref.dtype)
 
 
 def stay(x):
@@ -332,7 +332,7 @@
     expand_conv(taps_t, wt, True)
     for layer in range(w_track.shape[0]):
         for tap in range(3):
-            weight = w_track[layer, tap].astype(f32)
+            weight = 0.5 * w_track[layer, tap].astype(f32)
             rows = pl.ds(tap * 2 * LANES, 2 * LANES)
             wf[layer, rows, :] = expand_tap(weight).astype(wf.dtype)
             wb[layer, rows, :] = expand_tap(weight.T).astype(wb.dtype)
@@ -370,9 +370,11 @@
     )(*[stay(a) for a in sources])
 
 
-def silu_and_slope(v):
-    s = 0.5 * jnp.tanh(0.5 * v) + 0.5
-    return v * s, s * (1.0 + v * (1.0 - s))
+def silu_and_slope(u):
+    t = jnp.tanh(u)
+    double = 1.0 + t
+    silu = u * double
+    return silu, double + silu * (1.0 - t)
 
 
 def dot(a, b):
@@ -400,8 +402,9 @@
     low = low_half((rows, LANES))
     straight, crossed = None, None
     for pair in range(2):
-        even = [full[2 * pair * rows : (2 * pair + 1) * rows, (2 * h + pair) * LANES : (2 * h + pair + 1) * LANES] for h in range(2)]
-        odd = [full[(2 * pair + 1) * rows : (2 * pair + 2) * rows, (2 * h + pair) * LANES : (2 * h + pair + 1) * LANES] for h in range(2)]
+        tiles = [slice((2 * pair + h) * LANES, (2 * pair + h + 1) * LANES) for h in range(2)]
+        even = [full[2 * pair * rows : (2 * pair + 1) * rows, tile] for tile in tiles]
+        odd = [full[(2 * pair + 1) * rows : (2 * pair + 2) * rows, tile] for tile in tiles]
         direct = jnp.where(low, even[0], odd[1])
         swapped = jnp.where(low, even[1], odd[0])
         straight = direct if straight is None else straight + direct
@@ -409,48 +412,37 @@
     return straight + swap_halves(crossed)
 
 
-def step_kernel(
-    rows_total,
-    blocks,
-    margin,
-    loss_scale,
-    own,
-    dilation,
-    gathered,
-    w4,
-    wo4,
-    wc,
-    wt,
-    wf,
-    wb,
-    table_t,
-    prediction,
-    grad_in,
-    grad_conv,
-    grad_track,
-    grad_out_t,
-    grad_table_t,
-    pixels,
-    target,
-    meta,
-    proj,
-    mixed,
-    acts,
-    gates,
-    slopes,
-    backward,
-    shown,
-):
+TILES = tuple(slice(n * LANES, (n + 1) * LANES) for n in range(4))
+
+
+def step_kernel(rows_total, blocks, margin, loss_scale, layers, *refs):
+    own, dilation, gathered, w4, wo4, wc, wt, wf, wb, table_t = refs[:10]
+    prediction, grad_in, grad_conv, grad_track, grad_out_t, grad_table_t = refs[10:16]
+    pixels, target, meta, shown, side = refs[16:21]
+    rest = list(refs[21:])
+
+    def take(count):
+        taken = rest[:count]
+        del rest[:count]
+        return taken
+
+    proj, proj_side = take(2), take(1)[0]
+    mixed, mixed_side = take(2), take(1)[0]
+    acts = [take(2) for _ in range(layers + 1)]
+    gates = [take(2) for _ in range(layers)]
+    slopes = [take(2) for _ in range(layers + 1)]
+    backward = [take(2) for _ in range(layers + 1)]
+
     size = rows_total * blocks
     strips = gathered.shape[0]
     rows_local = rows_total // strips
-    layers = wf.shape[0]
     bf16 = jnp.bfloat16
     f32 = jnp.float32
     mine = own[0]
     bits = strips.bit_length() - 1
     local = rows_local * blocks
-    middle = pl.ds(margin * blocks, size)
+    inner = slice(blocks, blocks + size)
+    middle = slice(margin * blocks, margin * blocks + size)
 
     for s in range(strips):
         apart = mine ^ s
@@ -461,65 +453,69 @@
         target[pl.ds(s, rows_total, stride=blocks), :] = gathered[place, local : local + rows_total, :].astype(f32)
         meta[s : s + 1, :] = gathered[place, local + rows_total : local + rows_total + 8, :].astype(f32)[0:1]
 
-    for ref in (proj, mixed):
+    for ref in (*proj, proj_side, *mixed, mixed_side):
         ref[0:blocks, :] = jnp.zeros((blocks, ref.shape[1]), bf16)
-        ref[size + blocks : size + 2 * blocks, :] = jnp.zeros((blocks, ref.shape[1]), bf16)
-    edge = jnp.zeros((margin * blocks, acts.shape[2]), bf16)
-    for layer in range(layers):
-        acts[layer, 0 : margin * blocks, :] = edge
-        acts[layer, margin * blocks + size :, :] = edge
-    gates[0 : margin * blocks, :] = edge
-    gates[margin * blocks + size :, :] = edge
-
-    low = low_half((size, LANES))
-    position = lax.broadcasted_iota(jnp.int32, (size, LANES), 0) % blocks
-    outside = jnp.where(low, blocks - 1, 0)
-    keep = position != outside
-
-    def put_padded(ref, value):
-        rounded = value.astype(bf16)
-        ref[blocks : blocks + size, 0 : 4 * LANES] = rounded
-        wide = rounded.astype(f32)
+        ref[size + blocks :, :] = jnp.zeros((blocks, ref.shape[1]), bf16)
+    edge = jnp.zeros((margin * blocks, 2 * LANES), bf16)
+    for ref in [ref for pair in acts[:layers] + gates for ref in pair]:
+        ref[0 : margin * blocks, :] = edge
+        ref[margin * blocks + size :, :] = edge
+    gap = jnp.zeros((rows_total, 8, LANES), f32)
+    side[:, :, 0:8, :] = jnp.broadcast_to(gap[None], (4, rows_total, 8, LANES))
+    side[:, :, 8 + blocks : 16 + blocks, :] = jnp.broadcast_to(gap[None], (4, rows_total, 8, LANES))
+
+    side_low = low_half((rows_total, blocks, LANES))
+
+    def put_side(ref, values):
         for h in range(2):
-            following = pltpu.roll(wide[:, 2 * h * LANES : (2 * h + 1) * LANES], size - 1, 0)
-            previous = pltpu.roll(wide[:, (2 * h + 1) * LANES : (2 * h + 2) * LANES], 1, 0)
-            side = jnp.where(keep, jnp.where(low, following, previous), 0.0)
-            ref[blocks : blocks + size, (4 + h) * LANES : (5 + h) * LANES] = side.astype(bf16)
-
-    def window(ref, h, i):
+            for pair in range(2):
+                side[2 * h + pair, :, 8 : 8 + blocks, :] = values[pair][:, TILES[h]].reshape(rows_total, blocks, LANES)
+            following = side[2 * h, :, 9 : 9 + blocks, :]
+            previous = side[2 * h + 1, :, 7 : 7 + blocks, :]
+            ref[inner, TILES[h]] = jnp.where(side_low, following, previous).reshape(size, LANES).astype(bf16)
+
+    def window(pairs, beside, h, i):
         rows = slice(i * blocks, i * blocks + size)
-        return [ref[rows, 2 * h * LANES : (2 * h + 2) * LANES], ref[rows, (4 + h) * LANES : (5 + h) * LANES]]
-
-    put_padded(proj, dot(pixels[...], w4[...]))
+        return [pairs[0][rows, TILES[h]], pairs[1][rows, TILES[h]], beside[rows, TILES[h]]]
+
+    def windows(pairs, beside, h):
+        return jnp.concatenate([piece for i in range(3) for piece in window(pairs, beside, h, i)], axis=1)
+
+    projected = dot(pixels[...], w4[...])
+    projected = [projected[:, 0 : 2 * LANES], projected[:, 2 * LANES :]]
+    for pair in range(2):
+        proj[pair][inner, :] = projected[pair].astype(bf16)
+    put_side(proj_side, projected)
     for h in range(2):
-        lanes = slice(2 * h * LANES, (2 * h + 2) * LANES)
-        left = jnp.concatenate([piece for i in range(3) for piece in window(proj, h, i)], axis=1)
-        silu, slope = silu_and_slope(dot(left, wc[h]))
-        slopes[layers, :, lanes] = slope
-        centre = proj[blocks : blocks + size, lanes].astype(f32)
-        acts[0, middle, lanes] = (centre + silu).astype(bf16)
-
-    def tap_window(ref, spacing, sign, pair):
+        silu, slope = silu_and_slope(dot(windows(proj, proj_side, h), wc[h]))
+        for pair in range(2):
+            slopes[layers][pair][:, TILES[h]] = slope[:, TILES[pair]]
+            centre = proj[pair][inner, TILES[h]].astype(f32)
+            acts[0][pair][middle, TILES[h]] = (centre + silu[:, TILES[pair]]).astype(bf16)
+
+    def tap_rows(ref, layer, sign):
         pieces = []
         for tap in range(3):
-            start = pl.multiple_of((margin + sign * (tap - 1) * spacing) * blocks, 16)
-            for h in range(2):
-                pieces.append(ref[pl.ds(start, size), (2 * h + pair) * LANES : (2 * h + pair + 1) * LANES])
+            if tap == 1:
+                pieces.append(ref[middle, :])
+            else:
+                start = pl.multiple_of((margin + sign * (tap - 1) * dilation[layer]) * blocks, 16)
+                pieces.append(ref[pl.ds(start, size), :])
         return jnp.concatenate(pieces, axis=1)
 
-    def forward(layer, carry):
-        spacing = dilation[layer]
+    def track(layer, pair):
+        return dot(tap_rows(acts[layer][pair], layer, 1), wf[layer])
+
+    sums = [track(0, pair) for pair in range(2)]
+    for layer in range(layers):
         for pair in range(2):
-            silu, slope = silu_and_slope(dot(tap_window(acts.at[layer], spacing, 1, pair), wf[layer]))
-            for h in range(2):
-                lanes = slice((2 * h + pair) * LANES, (2 * h + pair + 1) * LANES)
-                part = slice(h * LANES, (h + 1) * LANES)
-                slopes[layer, :, lanes] = slope[:, part]
-                centre = acts[layer, middle, lanes].astype(f32)
-                acts[layer + 1, middle, lanes] = (centre + silu[:, part]).astype(bf16)
-        return carry
-
-    lax.fori_loop(0, layers, forward, 0)
+            silu, slope = silu_and_slope(sums[pair])
+            slopes[layer][pair][...] = slope
+            centre = acts[layer][pair][middle, :].astype(f32)
+            rows = middle if layer + 1 < layers else slice(0, size)
+            acts[layer + 1][pair][rows, :] = (centre + silu).astype(bf16)
+            if layer + 1 < layers:
+                sums[pair] = track(layer + 1, pair)
 
     det_count = table_t.shape[1] // (3 * SLOTS)
     meta_b = meta[...].astype(bf16)
@@ -533,15 +529,17 @@
     flag = dot(meta_b, jnp.where(source == slot_of + 2 * SLOTS, 1.0, 0.0).astype(bf16))
     offsets = dot_nt(jnp.concatenate([selector] * 3, axis=1), table_t[...]) * flag
 
-    raw = dot_nt(acts[layers, middle, :], wo4[...]).reshape(rows_total, blocks, LANES) + offsets[None]
+    last = jnp.concatenate([ref[...] for ref in acts[layers]], axis=1)
+    raw = dot_nt(last, wo4[...]).reshape(rows_total, blocks, LANES) + offsets[None]
     rounded = raw.astype(bf16).astype(f32)
     shown[...] = rounded.reshape(size, LANES)
     prediction[...] = shown[pl.ds(mine, rows_total, stride=blocks), :].astype(bf16)
     residue = (rounded - target[...].reshape(rows_total, blocks, LANES)) * loss_scale
     column_sums = jnp.sum(residue, axis=0) * flag
     residue_b = residue.reshape(size, LANES).astype(bf16)
-    backward[...] = dot(residue_b, wo4[...])
-    grad_out_t[...] = band_diagonal(dot_tn(residue_b, acts[layers, middle, :]))
+    for pair in range(2):
+        backward[layers][pair][...] = dot(residue_b, wo4[:, 2 * pair * LANES : (2 * pair + 2) * LANES])
+    grad_out_t[...] = band_diagonal(dot_tn(residue_b, last))
     sums = jnp.concatenate(thirds(column_sums), axis=0)
     full = dot_tn(sums, jnp.concatenate([selector] * 3, axis=0))
     band_count = LANES // SLOTS
@@ -550,26 +548,15 @@
     )
 
     tap_low = low_half((HALF, LANES))
-
-    def back(step, carry):
-        layer = layers - 1 - step
-        spacing = dilation[layer]
-        gates[middle, :] = (backward[...] * slopes[layer]).astype(bf16)
+    for layer in reversed(range(layers)):
         moved = []
         for pair in range(2):
-            right = tap_window(gates, spacing, -1, pair)
+            gates[layer][pair][middle, :] = (backward[layer + 1][pair][...] * slopes[layer][pair][...]).astype(bf16)
+            right = tap_rows(gates[layer][pair], layer, -1)
             moved.append(right)
-            update = dot(right, wb[layer])
-            for h in range(2):
-                lanes = slice((2 * h + pair) * LANES, (2 * h + pair + 1) * LANES)
-                backward[:, lanes] = backward[:, lanes] + update[:, h * LANES : (h + 1) * LANES]
-        left = [
-            jnp.concatenate(
-                [acts[layer, middle, (2 * h + pair) * LANES : (2 * h + pair + 1) * LANES] for h in range(2)], axis=1
-            )
-            for pair in range(2)
-        ]
-        full = dot_tn(jnp.concatenate(left, axis=0), jnp.concatenate(moved, axis=0))
+            backward[layer][pair][...] = backward[layer + 1][pair][...] + dot(right, wb[layer])
+        left = jnp.concatenate([acts[layer][pair][middle, :] for pair in range(2)], axis=0)
+        full = dot_tn(left, jnp.concatenate(moved, axis=0))
         for tap in range(3):
             first = full[:, 2 * tap * LANES : (2 * tap + 1) * LANES]
             second = full[:, (2 * tap + 1) * LANES : (2 * tap + 2) * LANES]
@@ -578,26 +565,31 @@
                 lower = slice((2 * h + 1) * HALF, (2 * h + 2) * HALF)
                 straight = jnp.where(tap_low, first[upper], second[lower])
                 crossed = jnp.where(tap_low, second[upper], first[lower])
-                start = pl.multiple_of((layer * 3 + tap) * LANES, LANES) + h * HALF
-                grad_track[pl.ds(start, HALF), :] = straight + swap_halves(crossed)
-        return carry
-
-    lax.fori_loop(0, layers, back, 0)
-
-    feature_grad = backward[...].astype(bf16).astype(f32)
-    put_padded(mixed, feature_grad * slopes[layers])
-    lifted = []
+                start = (layer * 3 + tap) * LANES + h * HALF
+                grad_track[start : start + HALF, :] = 0.5 * (straight + swap_halves(crossed))
+
+    gradients = [backward[0][pair][...].astype(bf16).astype(f32) for pair in range(2)]
+    values = [gradients[pair] * slopes[layers][pair][...] for pair in range(2)]
+    for pair in range(2):
+        mixed[pair][inner, :] = values[pair].astype(bf16)
+    put_side(mixed_side, values)
+    lifted = [[None, None], [None, None]]
     for h in range(2):
-        lanes = slice(2 * h * LANES, (2 * h + 2) * LANES)
-        left = jnp.concatenate([piece for i in range(3) for piece in window(mixed, h, i)], axis=1)
-        lifted.append((backward[:, lanes].astype(bf16).astype(f32) + dot(left, wt[h])).astype(bf16))
-    grad_in[...] = band_diagonal(dot_tn(pixels[...], jnp.concatenate(lifted, axis=1)))
+        pulled = dot(windows(mixed, mixed_side, h), wt[h])
+        for pair in range(2):
+            centre = backward[0][pair][:, TILES[h]].astype(bf16).astype(f32)
+            lifted[pair][h] = (centre + pulled[:, TILES[pair]]).astype(bf16)
+    grad_in[...] = band_diagonal(dot_tn(pixels[...], jnp.concatenate(lifted[0] + lifted[1], axis=1)))
 
     width = grad_conv.shape[1]
     for h in range(2):
-        left = jnp.concatenate(window(proj, h, 1), axis=1)
+        left = jnp.concatenate(window(proj, proj_side, h, 1), axis=1)
         right = jnp.concatenate(
-            [mixed[(2 - i) * blocks : (2 - i) * blocks + size, 2 * h * LANES : (2 * h + 2) * LANES] for i in range(3)],
+            [
+                mixed[pair][(2 - i) * blocks : (2 - i) * blocks + size, TILES[h]]
+                for i in range(3)
+                for pair in range(2)
+            ],
             axis=1,
         )
         full = dot_tn(left, right)
@@ -608,7 +600,7 @@
                     row = INPUT_SLOTS.index(out_slot + j - 1) * HALF
                     tile = 2 * i + out_slot // 2
                     parts.append(full[row : row + HALF, tile * LANES : (tile + 1) * LANES])
-                total = parts[0] + parts[2] + swap_halves(parts[1] + parts[3])
+                total = 0.5 * (parts[0] + parts[2] + swap_halves(parts[1] + parts[3]))
                 for g in range(2):
                     start = ((3 * i + j) * 4 + 2 * h + g) * width
                     piece = total[g * width : (g + 1) * width]
@@ -618,7 +610,6 @@
 
 
 def replicated_step(gathered, own, weights, w_track_shape, w_conv_shape, table_shape, dilation, rows_total, blocks):
-    strips = gathered.shape[0]
     layers = w_track_shape[0]
     margin = rows_total // 4
     size = rows_total * blocks
@@ -629,8 +620,11 @@
     vmem = pl.BlockSpec(memory_space=pltpu.VMEM)
     f32, bf16 = jnp.float32, jnp.bfloat16
     taps = math.prod(w_conv_shape[:4])
+    wide = 2 * LANES
+    ringed = pltpu.VMEM((size + 2 * blocks, wide), bf16)
+    spaced = pltpu.VMEM((size + 2 * margin * blocks, wide), bf16)
     outs = pl.pallas_call(
-        lambda *refs: step_kernel(rows_total, blocks, margin, loss_scale, *refs),
+        lambda *refs: step_kernel(rows_total, blocks, margin, loss_scale, layers, *refs),
         out_shape=(
             jax.ShapeDtypeStruct((rows_total, LANES), bf16),
             jax.ShapeDtypeStruct((band_count, chan_count), f32),
@@ -645,14 +639,14 @@
             pltpu.VMEM((size, LANES), bf16),
             pltpu.VMEM((size, LANES), f32),
             pltpu.VMEM((blocks, LANES), f32),
-            pltpu.VMEM((size + 2 * blocks, 6 * LANES), bf16),
-            pltpu.VMEM((size + 2 * blocks, 6 * LANES), bf16),
-            pltpu.VMEM((layers + 1, size + 2 * margin * blocks, 4 * LANES), bf16),
-            pltpu.VMEM((size + 2 * margin * blocks, 4 * LANES), bf16),
-            pltpu.VMEM((layers + 1, size, 4 * LANES), f32),
-            pltpu.VMEM((size, 4 * LANES), f32),
             pltpu.VMEM((size, LANES), f32),
-        ],
+            pltpu.VMEM((4, rows_total, blocks + 16, LANES), f32),
+        ]
+        + [ringed] * 6
+        + [spaced] * (2 * layers)
+        + [pltpu.VMEM((size, wide), bf16)] * 2
+        + [spaced] * (2 * layers)
+        + [pltpu.VMEM((size, wide), f32)] * (4 * (layers + 1)),
         compiler_params=pltpu.CompilerParams(vmem_limit_bytes=STEP_VMEM),
         interpret=INTERPRET,
         name="strip_step",

time: 30.3 us -> 27.5 us (0.908)
  Pallas kernels: 15.7 us -> 13 us
    pallas_call x1, Pallas kernels: 12.8 us -> 10 us  [replicated_step(): pl.pallas_call(lambda *refs: step_kernel(rows_total, blocks, margin, loss...]
  transfers between devices with their start and end apart: 4 -> 4, of which waited for: 4 -> 3; matrix products, arithmetic and copies ran while one was open for 0% -> 0% of each run, Pallas kernels for 7% -> 8%
where the time goes in v3:
time: 27.5 us; the launch traced here: 27.3 us
  Pallas kernels  13 us (47%)
  starting transfers between devices  8.01 us (29%)
  waiting for transfers between devices  5.57 us (20%)
  between operations  0.71 us (3%)
    pallas_call x1, Pallas kernels, replicated_step(): pl.pallas_call(lambda *refs: step_kernel(rows_total, blocks, margin, loss...  10 us
    ppermute x4, starting transfers between devices, gather_strip(): held = jnp.concatenate([held, lax.ppermute(held, 'strip', pairs)], axis=0)  8.01 us
    ppermute x4, waiting for transfers between devices, gather_strip(): held = jnp.concatenate([held, lax.ppermute(held, 'strip', pairs)], axis=0)  5.57 us
    pallas_call x1, Pallas kernels, prepare_weights(): pl.pallas_call(prepare_kernel, out_shape=tuple((jax.ShapeDtypeStruct(s, j...  2.08 us
    pallas_call x1, Pallas kernels, device_payload(): pl.pallas_call(payload_kernel, out_shape=jax.ShapeDtypeStruct((local + ta...  0.86 us
  transfers between devices with their start and end apart: 4, of which 3 were waited for; matrix products, arithmetic and copies ran while one was open for 0% of the time, Pallas kernels for 8%

profile of v3, /device:TPU:0, one launch (start us, length us, event | category | flops | bytes accessed | tf_op | source)
XLA Modules:
  0.0 27.3 jit_solution(15861165711150551500)
XLA Ops:
  0.6 0.0 copy-start
  0.6 0.9 %payload.1 = bf16[72,128]{1,0:T(8,128)(2,1)S(1)} custom-call(bf16[2,2048]{1,0:T(2,128)(2,1)} %refs_0_.2, bf16[32,128]{1,0:T(8,128)(2,1)} %refs_1_.2, s32[4]{0:T(128)} %refs_2_.2, s32[4]{0:T(128)} %refs_3_.1), custom_call_target="tpu_custom_call" | custom-call | tf_op jit(solution)/shard_map/payload/pallas_call | solution.py:690
  1.5 4.1 %collective-permute-start = (bf16[1,72,128]{2,1,0:T(8,128)(2,1)S(1)}, bf16[1,72,128]{2,1,0:T(8,128)(2,1)S(1)}, u32[]{:S(2)}, u32[]{:S(2)}) collective-permute-start(bf16[1,72,128]{2,1,0:T(8,128)(2,1)S(1)} %bitcast.10), channel_id=1, source_target_pairs={{0,8},{1,9},{2,10},{3,11},{4,12},{5,13},{6,14},{7,15},{8,0},{9,1},... | collective-permute-start | bytes 55304 | tf_op jit(solution)/shard_map/ppermute | solution.py:714
  5.6 1.7 %collective-permute-done = bf16[1,72,128]{2,1,0:T(8,128)(2,1)S(1)} collective-permute-done((bf16[1,72,128]{2,1,0:T(8,128)(2,1)S(1)}, bf16[1,72,128]{2,1,0:T(8,128)(2,1)S(1)}, u32[]{:S(2)}, u32[]{:S(2)}) %collective-permute-start) | collective-permute-done | bytes 18464 | tf_op jit(solution)/shard_map/ppermute | solution.py:714
  7.4 1.9 %collective-permute-start.1 = (bf16[2,72,128]{2,1,0:T(8,128)(2,1)S(1)}, bf16[2,72,128]{2,1,0:T(8,128)(2,1)S(1)}, u32[]{:S(2)}, u32[]{:S(2)}) collective-permute-start(bf16[2,72,128]{2,1,0:T(8,128)(2,1)S(1)} %pad_maximum_fusion.2), channel_id=1, source_target_pairs={{0,4},{1,5},{2,6},{3,7},{4,0},{5,1},{6,2},{7,3},{8,12},{9,13},{10,... | collective-permute-start | bytes 110600 | tf_op jit(solution)/shard_map/ppermute | solution.py:714
  9.3 2.1 %prepare_weights.1 = (bf16[128,512]{1,0:T(8,128)(2,1)S(1)}, bf16[128,512]{1,0:T(8,128)(2,1)S(1)}, bf16[2,1152,256]{2,1,0:T(8,128)(2,1)S(1)}, bf16[2,1152,256]{2,...) custom-call(bf16[3,3,128,128]{3,2,1,0:T(8,128)(2,1)} %refs_0_.3, ...), custom_call_target="tpu_custom_call" | custom-call | tf_op jit(solution)/shard_map/prepare_weights/pallas_call | solution.py:362
  11.4 0.0 collective-permute-done.1
  11.4 1.9 %collective-permute-start.2 = (bf16[4,72,128]{2,1,0:T(8,128)(2,1)S(1)}, bf16[4,72,128]{2,1,0:T(8,128)(2,1)S(1)}, u32[]{:S(2)}, u32[]{:S(2)}) collective-permute-start(bf16[4,72,128]{2,1,0:T(8,128)(2,1)S(1)} %pad_maximum_fusion.1), channel_id=1, source_target_pairs={{0,2},{1,3},{2,0},{3,1},{4,6},{5,7},{6,4},{7,5},{8,10},{9,11},{10,... | collective-permute-start | bytes 221192 | tf_op jit(solution)/shard_map/ppermute | solution.py:714
  13.3 2.5 %collective-permute-done.2 = bf16[4,72,128]{2,1,0:T(8,128)(2,1)S(1)} collective-permute-done((bf16[4,72,128]{2,1,0:T(8,128)(2,1)S(1)}, bf16[4,72,128]{2,1,0:T(8,128)(2,1)S(1)}, u32[]{:S(2)}, u32[]{:S(2)}) %collective-permute-start.2) | collective-permute-done | bytes 73760 | tf_op jit(solution)/shard_map/ppermute | solution.py:714
  15.9 0.1 collective-permute-start.3
  16.0 1.3 %collective-permute-done.3 = bf16[8,72,128]{2,1,0:T(8,128)(2,1)S(1)} collective-permute-done((bf16[8,72,128]{2,1,0:T(8,128)(2,1)S(1)}, bf16[8,72,128]{2,1,0:T(8,128)(2,1)S(1)}, u32[]{:S(2)}, u32[]{:S(2)}) %collective-permute-start.3) | collective-permute-done | bytes 147488 | tf_op jit(solution)/shard_map/ppermute | solution.py:714
  17.3 0.0 copy-done
  17.3 10.0 %strip_step.1 = (bf16[32,128]{1,0:T(8,128)(2,1)}, f32[32,128]{1,0:T(8,128)}, f32[1152,32]{1,0:T(8,128)}, f32[1152,128]{1,0:T(8,128)}, f32[32,128]{1,0:T(8,128)}, /*index=5*/f32[32,64]{1,0:T(8,128)}) custom-call(s32[1]{0:T(128)} %bitcast.refs_0_, s32[3]{0:T(128)S(1)} %copy-done, bf16[16,72,128]{2,1,0:T(8,128)(2,1)S(1)} %constant_dynamic-update-slice_fusion.refs_2_, ...), custom_call_target="tpu_custom_call" | custom-call | tf_op jit(solution)/shard_map/strip_step/pallas_call | solution.py:626
  (8 shorter events, 0.1 us)
Async XLA Ops:
  0.6 16.7 %copy-start = (s32[3]{0:T(128)S(1)}, s32[3]{0:T(128)}, u32[]{:S(2)}) copy-start(s32[3]{0:T(128)} %refs_1_.3) | copy-start | bytes 40
  1.5 5.9 %collective-permute-start = (bf16[1,72,128]{2,1,0:T(8,128)(2,1)S(1)}, bf16[1,72,128]{2,1,0:T(8,128)(2,1)S(1)}, u32[]{:S(2)}, u32[]{:S(2)}) collective-permute-start(bf16[1,72,128]{2,1,0:T(8,128)(2,1)S(1)} %bitcast.10), channel_id=1, source_target_pairs={{0,8},{1,9},{2,10},{3,11},{4,12},{5,13},{6,14},{7,15},{8,0},{9,1},... | collective-permute-start | bytes 55304 | tf_op jit(solution)/shard_map/ppermute | solution.py:714
  7.4 4.0 %collective-permute-start.1 = (bf16[2,72,128]{2,1,0:T(8,128)(2,1)S(1)}, bf16[2,72,128]{2,1,0:T(8,128)(2,1)S(1)}, u32[]{:S(2)}, u32[]{:S(2)}) collective-permute-start(bf16[2,72,128]{2,1,0:T(8,128)(2,1)S(1)} %pad_maximum_fusion.2), channel_id=1, source_target_pairs={{0,4},{1,5},{2,6},{3,7},{4,0},{5,1},{6,2},{7,3},{8,12},{9,13},{10,... | collective-permute-start | bytes 110600 | tf_op jit(solution)/shard_map/ppermute | solution.py:714
  11.4 4.4 %collective-permute-start.2 = (bf16[4,72,128]{2,1,0:T(8,128)(2,1)S(1)}, bf16[4,72,128]{2,1,0:T(8,128)(2,1)S(1)}, u32[]{:S(2)}, u32[]{:S(2)}) collective-permute-start(bf16[4,72,128]{2,1,0:T(8,128)(2,1)S(1)} %pad_maximum_fusion.1), channel_id=1, source_target_pairs={{0,2},{1,3},{2,0},{3,1},{4,6},{5,7},{6,4},{7,5},{8,10},{9,11},{10,... | collective-permute-start | bytes 221192 | tf_op jit(solution)/shard_map/ppermute | solution.py:714
  15.9 1.4 %collective-permute-start.3 = (bf16[8,72,128]{2,1,0:T(8,128)(2,1)S(1)}, bf16[8,72,128]{2,1,0:T(8,128)(2,1)S(1)}, u32[]{:S(2)}, u32[]{:S(2)}) collective-permute-start(bf16[8,72,128]{2,1,0:T(8,128)(2,1)S(1)} %pad_maximum_fusion), channel_id=1, source_target_pairs={{0,1},{1,0},{2,3},{3,2},{4,5},{5,4},{6,7},{7,6},{8,9},{9,8},{10,11... | collective-permute-start | bytes 442376 | tf_op jit(solution)/shard_map/ppermute | solution.py:714

commit v4 on v3

--- a/solution.py
+++ b/solution.py
@@ -1,3 +1,4 @@
+import functools
 import math
 
 import jax
@@ -370,11 +371,14 @@
     )(*[stay(a) for a in sources])
 
 
-def silu_and_slope(u):
+def silu_of(u):
+    return u * (1.0 + jnp.tanh(u))
+
+
+def double_slope(u):
     t = jnp.tanh(u)
     double = 1.0 + t
-    silu = u * double
-    return silu, double + silu * (1.0 - t)
+    return double + u * double * (1.0 - t)
 
 
 def dot(a, b):
@@ -415,11 +419,11 @@
 TILES = tuple(slice(n * LANES, (n + 1) * LANES) for n in range(4))
 
 
-def step_kernel(rows_total, blocks, margin, loss_scale, layers, *refs):
-    own, dilation, gathered, w4, wo4, wc, wt, wf, wb, table_t = refs[:10]
-    prediction, grad_in, grad_conv, grad_track, grad_out_t, grad_table_t = refs[10:16]
-    pixels, target, meta, shown, side = refs[16:21]
-    rest = list(refs[21:])
+def step_kernel(rows_total, blocks, margin, loss_scale, layers, position, *refs):
+    spacing_in, gathered, w4, wo4, wc, wt, wf, wb, table_t = refs[:9]
+    prediction, grad_in, grad_conv, grad_track, grad_out_t, grad_table_t = refs[9:15]
+    pixels, target, meta, shown, side, dilation, arrived = refs[15:22]
+    rest = list(refs[22:])
 
     def take(count):
         taken = rest[:count]
@@ -430,7 +434,7 @@
     mixed, mixed_side = take(2), take(1)[0]
     acts = [take(2) for _ in range(layers + 1)]
     gates = [take(2) for _ in range(layers)]
-    slopes = [take(2) for _ in range(layers + 1)]
+    halves = [take(2) for _ in range(layers + 1)]
     backward = [take(2) for _ in range(layers + 1)]
 
     size = rows_total * blocks
@@ -438,7 +442,9 @@
     rows_local = rows_total // strips
     bf16 = jnp.bfloat16
     f32 = jnp.float32
-    mine = own[0]
+    mine = position if INTERPRET else lax.axis_index("strip")
+    scalars = pltpu.make_async_copy(spacing_in, dilation, arrived)
+    scalars.start()
     bits = strips.bit_length() - 1
     local = rows_local * blocks
     inner = slice(blocks, blocks + size)
@@ -464,6 +470,8 @@
     side[:, :, 0:8, :] = jnp.broadcast_to(gap[None], (4, rows_total, 8, LANES))
     side[:, :, 8 + blocks : 16 + blocks, :] = jnp.broadcast_to(gap[None], (4, rows_total, 8, LANES))
 
+    scalars.wait()
+    zero = pl.multiple_of((dilation[0] >> 16) * 8, 8)
     side_low = low_half((rows_total, blocks, LANES))
 
     def put_side(ref, values):
@@ -487,9 +495,11 @@
         proj[pair][inner, :] = projected[pair].astype(bf16)
     put_side(proj_side, projected)
     for h in range(2):
-        silu, slope = silu_and_slope(dot(windows(proj, proj_side, h), wc[h]))
+        left = windows(proj, proj_side, h)
+        u = jnp.concatenate([dot(left[: size // 2], wc[h]), dot(left[size // 2 :], wc[h])], axis=0)
+        silu = silu_of(u)
         for pair in range(2):
-            slopes[layers][pair][:, TILES[h]] = slope[:, TILES[pair]]
+            halves[layers][pair][pl.ds(zero, size), TILES[h]] = u[:, TILES[pair]]
             centre = proj[pair][inner, TILES[h]].astype(f32)
             acts[0][pair][middle, TILES[h]] = (centre + silu[:, TILES[pair]]).astype(bf16)
 
@@ -503,19 +513,23 @@
                 pieces.append(ref[pl.ds(start, size), :])
         return jnp.concatenate(pieces, axis=1)
 
+    def forward(layer):
+        rows = middle if layer + 1 < layers else slice(0, size)
+        for pair in range(2):
+            part = sums[pair]
+            halves[layer][pair][pl.ds(zero, size), :] = part
+            centre = acts[layer][pair][middle, :].astype(f32)
+            acts[layer + 1][pair][rows, :] = (centre + silu_of(part)).astype(bf16)
+            if layer + 1 < layers:
+                sums[pair] = track(layer + 1, pair)
+
     def track(layer, pair):
-        return dot(tap_rows(acts[layer][pair], layer, 1), wf[layer])
+        left = tap_rows(acts[layer][pair], layer, 1)
+        return jnp.concatenate([dot(left[: size // 2], wf[layer]), dot(left[size // 2 :], wf[layer])], axis=0)
 
     sums = [track(0, pair) for pair in range(2)]
     for layer in range(layers):
-        for pair in range(2):
-            silu, slope = silu_and_slope(sums[pair])
-            slopes[layer][pair][...] = slope
-            centre = acts[layer][pair][middle, :].astype(f32)
-            rows = middle if layer + 1 < layers else slice(0, size)
-            acts[layer + 1][pair][rows, :] = (centre + silu).astype(bf16)
-            if layer + 1 < layers:
-                sums[pair] = track(layer + 1, pair)
+        forward(layer)
 
     det_count = table_t.shape[1] // (3 * SLOTS)
     meta_b = meta[...].astype(bf16)
@@ -540,23 +554,32 @@
     for pair in range(2):
         backward[layers][pair][...] = dot(residue_b, wo4[:, 2 * pair * LANES : (2 * pair + 2) * LANES])
     grad_out_t[...] = band_diagonal(dot_tn(residue_b, last))
-    sums = jnp.concatenate(thirds(column_sums), axis=0)
-    full = dot_tn(sums, jnp.concatenate([selector] * 3, axis=0))
+    parts = jnp.concatenate(thirds(column_sums), axis=0)
+    full = dot_tn(parts, jnp.concatenate([selector] * 3, axis=0))
     band_count = LANES // SLOTS
     grad_table_t[...] = sum(
         full[k * band_count : (k + 1) * band_count, k * det_count : (k + 1) * det_count] for k in range(SLOTS)
     )
 
     tap_low = low_half((HALF, LANES))
-    for layer in reversed(range(layers)):
+
+    def hold(layer, above):
+        for pair in range(2):
+            halves[layer][pair][pl.ds(zero + size, 8), 0:LANES] = backward[above][pair][0:8, 0:LANES]
+
+    def back(layer):
+        hold(layer, layer + 1)
         moved = []
         for pair in range(2):
-            gates[layer][pair][middle, :] = (backward[layer + 1][pair][...] * slopes[layer][pair][...]).astype(bf16)
+            gates[layer][pair][middle, :] = (backward[layer + 1][pair][...] * double_slope(halves[layer][pair][0:size, :])).astype(bf16)
             right = tap_rows(gates[layer][pair], layer, -1)
             moved.append(right)
-            backward[layer][pair][...] = backward[layer + 1][pair][...] + dot(right, wb[layer])
+        both = jnp.concatenate(moved, axis=0)
+        update = dot(both, wb[layer])
+        for pair in range(2):
+            backward[layer][pair][...] = backward[layer + 1][pair][...] + update[pair * size : (pair + 1) * size]
         left = jnp.concatenate([acts[layer][pair][middle, :] for pair in range(2)], axis=0)
-        full = dot_tn(left, jnp.concatenate(moved, axis=0))
+        full = dot_tn(left, both)
         for tap in range(3):
             first = full[:, 2 * tap * LANES : (2 * tap + 1) * LANES]
             second = full[:, (2 * tap + 1) * LANES : (2 * tap + 2) * LANES]
@@ -568,8 +591,12 @@
                 start = (layer * 3 + tap) * LANES + h * HALF
                 grad_track[start : start + HALF, :] = 0.5 * (straight + swap_halves(crossed))
 
+    for layer in reversed(range(layers)):
+        back(layer)
+
+    hold(layers, 0)
     gradients = [backward[0][pair][...].astype(bf16).astype(f32) for pair in range(2)]
-    values = [gradients[pair] * slopes[layers][pair][...] for pair in range(2)]
+    values = [gradients[pair] * double_slope(halves[layers][pair][0:size, :]) for pair in range(2)]
     for pair in range(2):
         mixed[pair][inner, :] = values[pair].astype(bf16)
     put_side(mixed_side, values)
@@ -609,22 +636,22 @@
                     grad_conv[start : start + width, :] = piece[:, :width]
 
 
-def replicated_step(gathered, own, weights, w_track_shape, w_conv_shape, table_shape, dilation, rows_total, blocks):
+def replicated_step(gathered, weights, w_track_shape, w_conv_shape, table_shape, dilation, rows_total, blocks, position=None):
     layers = w_track_shape[0]
     margin = rows_total // 4
     size = rows_total * blocks
     chan_count = w_track_shape[2]
     det_count, band_count = table_shape
     loss_scale = 1.0 / math.sqrt(rows_total * blocks * SLOTS)
-    smem = pl.BlockSpec(memory_space=pltpu.SMEM)
     vmem = pl.BlockSpec(memory_space=pltpu.VMEM)
+    hbm = pl.BlockSpec(memory_space=pltpu.HBM)
     f32, bf16 = jnp.float32, jnp.bfloat16
     taps = math.prod(w_conv_shape[:4])
     wide = 2 * LANES
     ringed = pltpu.VMEM((size + 2 * blocks, wide), bf16)
     spaced = pltpu.VMEM((size + 2 * margin * blocks, wide), bf16)
     outs = pl.pallas_call(
-        lambda *refs: step_kernel(rows_total, blocks, margin, loss_scale, layers, *refs),
+        lambda *refs: step_kernel(rows_total, blocks, margin, loss_scale, layers, position, *refs),
         out_shape=(
             jax.ShapeDtypeStruct((rows_total, LANES), bf16),
             jax.ShapeDtypeStruct((band_count, chan_count), f32),
@@ -633,7 +660,7 @@
             jax.ShapeDtypeStruct((band_count, chan_count), f32),
             jax.ShapeDtypeStruct((band_count, det_count), f32),
         ),
-        in_specs=[smem, smem] + [vmem] * 8,
+        in_specs=[hbm] + [vmem] * 8,
         out_specs=tuple([vmem] * 6),
         scratch_shapes=[
             pltpu.VMEM((size, LANES), bf16),
@@ -641,16 +668,19 @@
             pltpu.VMEM((blocks, LANES), f32),
             pltpu.VMEM((size, LANES), f32),
             pltpu.VMEM((4, rows_total, blocks + 16, LANES), f32),
+            pltpu.SMEM(dilation.shape, dilation.dtype),
+            pltpu.SemaphoreType.DMA,
         ]
         + [ringed] * 6
         + [spaced] * (2 * layers)
         + [pltpu.VMEM((size, wide), bf16)] * 2
         + [spaced] * (2 * layers)
-        + [pltpu.VMEM((size, wide), f32)] * (4 * (layers + 1)),
+        + [pltpu.VMEM((size + 8, wide), f32)] * (2 * (layers + 1))
+        + [pltpu.VMEM((size, wide), f32)] * (2 * (layers + 1)),
         compiler_params=pltpu.CompilerParams(vmem_limit_bytes=STEP_VMEM),
         interpret=INTERPRET,
         name="strip_step",
-    )(own, dilation, gathered, *weights)
+    )(stay(dilation), gathered, *weights)
     prediction, grad_in, grad_conv, grad_track, grad_out_t, grad_table_t = outs
     return (
         prediction,
@@ -720,11 +750,10 @@
     size = lax.axis_size("strip")
     rows_total = bands.shape[0] * size
     blocks = bands.shape[1] // LANES
-    own = lax.axis_index("strip").astype(jnp.int32).reshape(1)
     weights = prepare_weights(w_in, w_conv, w_track, w_out, table)
     gathered = gather_strip(device_payload(bands, target, detector, flags, blocks), size)
     return replicated_step(
-        gathered, own, weights, w_track.shape, w_conv.shape, table.shape, dilation, rows_total, blocks
+        gathered, weights, w_track.shape, w_conv.shape, table.shape, dilation, rows_total, blocks
     )
 
 

time: 27.5 us -> 26.9 us (0.978)
  Pallas kernels: 13 us -> 12.3 us
    pallas_call x1, Pallas kernels: 10 us -> 9.33 us  [replicated_step(): pl.pallas_call(lambda *refs: step_kernel(rows_total, blocks, margin, loss...]
where the time goes in v4:
time: 26.9 us; the launch traced here: 26.6 us
  Pallas kernels  12.3 us (46%)
  starting transfers between devices  8.01 us (30%)
  waiting for transfers between devices  5.57 us (21%)
  between operations  0.69 us (3%)
    pallas_call x1, Pallas kernels, replicated_step(): pl.pallas_call(lambda *refs: step_kernel(rows_total, blocks, margin, loss...  9.33 us
    ppermute x4, starting transfers between devices, gather_strip(): held = jnp.concatenate([held, lax.ppermute(held, 'strip', pairs)], axis=0)  8.01 us
    ppermute x4, waiting for transfers between devices, gather_strip(): held = jnp.concatenate([held, lax.ppermute(held, 'strip', pairs)], axis=0)  5.57 us
    pallas_call x1, Pallas kernels, prepare_weights(): pl.pallas_call(prepare_kernel, out_shape=tuple((jax.ShapeDtypeStruct(s, j...  2.08 us
    pallas_call x1, Pallas kernels, device_payload(): pl.pallas_call(payload_kernel, out_shape=jax.ShapeDtypeStruct((local + ta...  0.86 us
  transfers between devices with their start and end apart: 4, of which 3 were waited for; matrix products, arithmetic and copies ran while one was open for 0% of the time, Pallas kernels for 8%

profile of v4, /device:TPU:0, one launch (start us, length us, event | category | flops | bytes accessed | tf_op | source)
XLA Modules:
  0.0 26.6 jit_solution(1057259729298433426)
XLA Ops:
  0.6 0.9 %payload.1 = bf16[72,128]{1,0:T(8,128)(2,1)S(1)} custom-call(bf16[2,2048]{1,0:T(2,128)(2,1)} %refs_0_.3, bf16[32,128]{1,0:T(8,128)(2,1)} %refs_1_.1, s32[4]{0:T(128)} %refs_2_.2, s32[4]{0:T(128)} %refs_3_.1), custom_call_target="tpu_custom_call" | custom-call | tf_op jit(solution)/shard_map/payload/pallas_call | solution.py:720
  1.5 4.1 %collective-permute-start = (bf16[1,72,128]{2,1,0:T(8,128)(2,1)S(1)}, bf16[1,72,128]{2,1,0:T(8,128)(2,1)S(1)}, u32[]{:S(2)}, u32[]{:S(2)}) collective-permute-start(bf16[1,72,128]{2,1,0:T(8,128)(2,1)S(1)} %bitcast.9), channel_id=1, source_target_pairs={{0,8},{1,9},{2,10},{3,11},{4,12},{5,13},{6,14},{7,15},{8,0},{9,1},... | collective-permute-start | bytes 55304 | tf_op jit(solution)/shard_map/ppermute | solution.py:744
  5.6 1.7 %collective-permute-done = bf16[1,72,128]{2,1,0:T(8,128)(2,1)S(1)} collective-permute-done((bf16[1,72,128]{2,1,0:T(8,128)(2,1)S(1)}, bf16[1,72,128]{2,1,0:T(8,128)(2,1)S(1)}, u32[]{:S(2)}, u32[]{:S(2)}) %collective-permute-start) | collective-permute-done | bytes 18464 | tf_op jit(solution)/shard_map/ppermute | solution.py:744
  7.4 1.9 %collective-permute-start.1 = (bf16[2,72,128]{2,1,0:T(8,128)(2,1)S(1)}, bf16[2,72,128]{2,1,0:T(8,128)(2,1)S(1)}, u32[]{:S(2)}, u32[]{:S(2)}) collective-permute-start(bf16[2,72,128]{2,1,0:T(8,128)(2,1)S(1)} %pad_maximum_fusion.2), channel_id=1, source_target_pairs={{0,4},{1,5},{2,6},{3,7},{4,0},{5,1},{6,2},{7,3},{8,12},{9,13},{10,... | collective-permute-start | bytes 110600 | tf_op jit(solution)/shard_map/ppermute | solution.py:744
  9.3 2.1 %prepare_weights.1 = (bf16[128,512]{1,0:T(8,128)(2,1)S(1)}, bf16[128,512]{1,0:T(8,128)(2,1)S(1)}, bf16[2,1152,256]{2,1,0:T(8,128)(2,1)S(1)}, bf16[2,1152,256]{2,...) custom-call(bf16[3,3,128,128]{3,2,1,0:T(8,128)(2,1)} %refs_0_.4, ...), custom_call_target="tpu_custom_call" | custom-call | tf_op jit(solution)/shard_map/prepare_weights/pallas_call | solution.py:363
  11.4 0.0 collective-permute-done.1
  11.4 1.9 %collective-permute-start.2 = (bf16[4,72,128]{2,1,0:T(8,128)(2,1)S(1)}, bf16[4,72,128]{2,1,0:T(8,128)(2,1)S(1)}, u32[]{:S(2)}, u32[]{:S(2)}) collective-permute-start(bf16[4,72,128]{2,1,0:T(8,128)(2,1)S(1)} %pad_maximum_fusion.1), channel_id=1, source_target_pairs={{0,2},{1,3},{2,0},{3,1},{4,6},{5,7},{6,4},{7,5},{8,10},{9,11},{10,... | collective-permute-start | bytes 221192 | tf_op jit(solution)/shard_map/ppermute | solution.py:744
  13.3 2.5 %collective-permute-done.2 = bf16[4,72,128]{2,1,0:T(8,128)(2,1)S(1)} collective-permute-done((bf16[4,72,128]{2,1,0:T(8,128)(2,1)S(1)}, bf16[4,72,128]{2,1,0:T(8,128)(2,1)S(1)}, u32[]{:S(2)}, u32[]{:S(2)}) %collective-permute-start.2) | collective-permute-done | bytes 73760 | tf_op jit(solution)/shard_map/ppermute | solution.py:744
  15.8 0.1 collective-permute-start.3
  16.0 1.3 %collective-permute-done.3 = bf16[8,72,128]{2,1,0:T(8,128)(2,1)S(1)} collective-permute-done((bf16[8,72,128]{2,1,0:T(8,128)(2,1)S(1)}, bf16[8,72,128]{2,1,0:T(8,128)(2,1)S(1)}, u32[]{:S(2)}, u32[]{:S(2)}) %collective-permute-start.3) | collective-permute-done | bytes 147488 | tf_op jit(solution)/shard_map/ppermute | solution.py:744
  17.3 9.3 %strip_step.1 = (bf16[32,128]{1,0:T(8,128)(2,1)}, f32[32,128]{1,0:T(8,128)}, f32[1152,32]{1,0:T(8,128)}, f32[1152,128]{1,0:T(8,128)}, f32[32,128]{1,0:T(8,128)}, /*index=5*/f32[32,64]{1,0:T(8,128)}) custom-call(s32[3]{0:T(128)} %refs_0_.5, bf16[16,72,128]{2,1,0:T(8,128)(2,1)S(1)} %constant_dynamic-update-slice_fusion.refs_1_, ...), custom_call_target="tpu_custom_call" | custom-call | tf_op jit(solution)/shard_map/strip_step/pallas_call | solution.py:653
  (8 shorter events, 0.1 us)
Async XLA Ops:
  1.5 5.9 %collective-permute-start = (bf16[1,72,128]{2,1,0:T(8,128)(2,1)S(1)}, bf16[1,72,128]{2,1,0:T(8,128)(2,1)S(1)}, u32[]{:S(2)}, u32[]{:S(2)}) collective-permute-start(bf16[1,72,128]{2,1,0:T(8,128)(2,1)S(1)} %bitcast.9), channel_id=1, source_target_pairs={{0,8},{1,9},{2,10},{3,11},{4,12},{5,13},{6,14},{7,15},{8,0},{9,1},... | collective-permute-start | bytes 55304 | tf_op jit(solution)/shard_map/ppermute | solution.py:744
  7.4 4.0 %collective-permute-start.1 = (bf16[2,72,128]{2,1,0:T(8,128)(2,1)S(1)}, bf16[2,72,128]{2,1,0:T(8,128)(2,1)S(1)}, u32[]{:S(2)}, u32[]{:S(2)}) collective-permute-start(bf16[2,72,128]{2,1,0:T(8,128)(2,1)S(1)} %pad_maximum_fusion.2), channel_id=1, source_target_pairs={{0,4},{1,5},{2,6},{3,7},{4,0},{5,1},{6,2},{7,3},{8,12},{9,13},{10,... | collective-permute-start | bytes 110600 | tf_op jit(solution)/shard_map/ppermute | solution.py:744
  11.4 4.4 %collective-permute-start.2 = (bf16[4,72,128]{2,1,0:T(8,128)(2,1)S(1)}, bf16[4,72,128]{2,1,0:T(8,128)(2,1)S(1)}, u32[]{:S(2)}, u32[]{:S(2)}) collective-permute-start(bf16[4,72,128]{2,1,0:T(8,128)(2,1)S(1)} %pad_maximum_fusion.1), channel_id=1, source_target_pairs={{0,2},{1,3},{2,0},{3,1},{4,6},{5,7},{6,4},{7,5},{8,10},{9,11},{10,... | collective-permute-start | bytes 221192 | tf_op jit(solution)/shard_map/ppermute | solution.py:744
  15.8 1.4 %collective-permute-start.3 = (bf16[8,72,128]{2,1,0:T(8,128)(2,1)S(1)}, bf16[8,72,128]{2,1,0:T(8,128)(2,1)S(1)}, u32[]{:S(2)}, u32[]{:S(2)}) collective-permute-start(bf16[8,72,128]{2,1,0:T(8,128)(2,1)S(1)} %pad_maximum_fusion), channel_id=1, source_target_pairs={{0,1},{1,0},{2,3},{3,2},{4,5},{5,4},{6,7},{7,6},{8,9},{9,8},{10,11... | collective-permute-start | bytes 442376 | tf_op jit(solution)/shard_map/ppermute | solution.py:744

commit v5 on v4

--- a/solution.py
+++ b/solution.py
@@ -421,7 +421,7 @@
 
 def step_kernel(rows_total, blocks, margin, loss_scale, layers, position, *refs):
     spacing_in, gathered, w4, wo4, wc, wt, wf, wb, table_t = refs[:9]
-    prediction, grad_in, grad_conv, grad_track, grad_out_t, grad_table_t = refs[9:15]
+    prediction, grad_in, grad_conv, track_out, grad_out_t, grad_table_t = refs[9:15]
     pixels, target, meta, shown, side, dilation, arrived = refs[15:22]
     rest = list(refs[22:])
 
@@ -436,6 +436,13 @@
     gates = [take(2) for _ in range(layers)]
     halves = [take(2) for _ in range(layers + 1)]
     backward = [take(2) for _ in range(layers + 1)]
+    grad_track, sent = take(2)
+    leaving = []
+
+    def send(source, target, part):
+        copy = pltpu.make_async_copy(source, target, sent.at[part])
+        copy.start()
+        leaving.append(copy)
 
     size = rows_total * blocks
     strips = gathered.shape[0]
@@ -590,6 +597,8 @@
                 crossed = jnp.where(tap_low, second[upper], first[lower])
                 start = (layer * 3 + tap) * LANES + h * HALF
                 grad_track[start : start + HALF, :] = 0.5 * (straight + swap_halves(crossed))
+        rows = slice(layer * 3 * LANES, (layer + 1) * 3 * LANES)
+        send(grad_track.at[rows], track_out.at[rows], layer)
 
     for layer in reversed(range(layers)):
         back(layer)
@@ -634,6 +643,8 @@
                     if g:
                         piece = pltpu.roll(piece, LANES - width, 1)
                     grad_conv[start : start + width, :] = piece[:, :width]
+    for copy in leaving:
+        copy.wait()
 
 
 def replicated_step(gathered, weights, w_track_shape, w_conv_shape, table_shape, dilation, rows_total, blocks, position=None):
@@ -661,7 +672,7 @@
             jax.ShapeDtypeStruct((band_count, det_count), f32),
         ),
         in_specs=[hbm] + [vmem] * 8,
-        out_specs=tuple([vmem] * 6),
+        out_specs=(vmem, vmem, vmem, hbm, vmem, vmem),
         scratch_shapes=[
             pltpu.VMEM((size, LANES), bf16),
             pltpu.VMEM((size, LANES), f32),
@@ -676,7 +687,8 @@
         + [pltpu.VMEM((size, wide), bf16)] * 2
         + [spaced] * (2 * layers)
         + [pltpu.VMEM((size + 8, wide), f32)] * (2 * (layers + 1))
-        + [pltpu.VMEM((size, wide), f32)] * (2 * (layers + 1)),
+        + [pltpu.VMEM((size, wide), f32)] * (2 * (layers + 1))
+        + [pltpu.VMEM((layers * 3 * chan_count, chan_count), f32), pltpu.SemaphoreType.DMA((layers,))],
         compiler_params=pltpu.CompilerParams(vmem_limit_bytes=STEP_VMEM),
         interpret=INTERPRET,
         name="strip_step",

time: 26.9 us -> 27 us (level)
  no operation moved by 1% of the time
where the time goes in v5:
time: 27 us; the launch traced here: 26.8 us
  Pallas kernels  12.4 us (46%)
  starting transfers between devices  8.01 us (30%)
  waiting for transfers between devices  5.57 us (21%)
  between operations  0.69 us (3%)
    pallas_call x1, Pallas kernels, replicated_step(): pl.pallas_call(lambda *refs: step_kernel(rows_total, blocks, margin, loss...  9.45 us
    ppermute x4, starting transfers between devices, gather_strip(): held = jnp.concatenate([held, lax.ppermute(held, 'strip', pairs)], axis=0)  8.01 us
    ppermute x4, waiting for transfers between devices, gather_strip(): held = jnp.concatenate([held, lax.ppermute(held, 'strip', pairs)], axis=0)  5.57 us
    pallas_call x1, Pallas kernels, prepare_weights(): pl.pallas_call(prepare_kernel, out_shape=tuple((jax.ShapeDtypeStruct(s, j...  2.08 us
    pallas_call x1, Pallas kernels, device_payload(): pl.pallas_call(payload_kernel, out_shape=jax.ShapeDtypeStruct((local + ta...  0.86 us
  transfers between devices with their start and end apart: 4, of which 3 were waited for; matrix products, arithmetic and copies ran while one was open for 0% of the time, Pallas kernels for 8%

profile of v5, /device:TPU:0, one launch (start us, length us, event | category | flops | bytes accessed | tf_op | source)
XLA Modules:
  0.0 26.8 jit_solution(1917437115945210550)
XLA Ops:
  0.6 0.9 %payload.1 = bf16[72,128]{1,0:T(8,128)(2,1)S(1)} custom-call(bf16[2,2048]{1,0:T(2,128)(2,1)} %refs_0_.3, bf16[32,128]{1,0:T(8,128)(2,1)} %refs_1_.1, s32[4]{0:T(128)} %refs_2_.2, s32[4]{0:T(128)} %refs_3_.1), custom_call_target="tpu_custom_call" | custom-call | tf_op jit(solution)/shard_map/payload/pallas_call | solution.py:732
  1.5 4.1 %collective-permute-start = (bf16[1,72,128]{2,1,0:T(8,128)(2,1)S(1)}, bf16[1,72,128]{2,1,0:T(8,128)(2,1)S(1)}, u32[]{:S(2)}, u32[]{:S(2)}) collective-permute-start(bf16[1,72,128]{2,1,0:T(8,128)(2,1)S(1)} %bitcast.9), channel_id=1, source_target_pairs={{0,8},{1,9},{2,10},{3,11},{4,12},{5,13},{6,14},{7,15},{8,0},{9,1},... | collective-permute-start | bytes 55304 | tf_op jit(solution)/shard_map/ppermute | solution.py:756
  5.6 1.7 %collective-permute-done = bf16[1,72,128]{2,1,0:T(8,128)(2,1)S(1)} collective-permute-done((bf16[1,72,128]{2,1,0:T(8,128)(2,1)S(1)}, bf16[1,72,128]{2,1,0:T(8,128)(2,1)S(1)}, u32[]{:S(2)}, u32[]{:S(2)}) %collective-permute-start) | collective-permute-done | bytes 18464 | tf_op jit(solution)/shard_map/ppermute | solution.py:756
  7.4 1.9 %collective-permute-start.1 = (bf16[2,72,128]{2,1,0:T(8,128)(2,1)S(1)}, bf16[2,72,128]{2,1,0:T(8,128)(2,1)S(1)}, u32[]{:S(2)}, u32[]{:S(2)}) collective-permute-start(bf16[2,72,128]{2,1,0:T(8,128)(2,1)S(1)} %pad_maximum_fusion.2), channel_id=1, source_target_pairs={{0,4},{1,5},{2,6},{3,7},{4,0},{5,1},{6,2},{7,3},{8,12},{9,13},{10,... | collective-permute-start | bytes 110600 | tf_op jit(solution)/shard_map/ppermute | solution.py:756
  9.3 2.1 %prepare_weights.1 = (bf16[128,512]{1,0:T(8,128)(2,1)S(1)}, bf16[128,512]{1,0:T(8,128)(2,1)S(1)}, bf16[2,1152,256]{2,1,0:T(8,128)(2,1)S(1)}, bf16[2,1152,256]{2,...) custom-call(bf16[3,3,128,128]{3,2,1,0:T(8,128)(2,1)} %refs_0_.4, ...), custom_call_target="tpu_custom_call" | custom-call | tf_op jit(solution)/shard_map/prepare_weights/pallas_call | solution.py:363
  11.4 0.0 collective-permute-done.1
  11.4 1.9 %collective-permute-start.2 = (bf16[4,72,128]{2,1,0:T(8,128)(2,1)S(1)}, bf16[4,72,128]{2,1,0:T(8,128)(2,1)S(1)}, u32[]{:S(2)}, u32[]{:S(2)}) collective-permute-start(bf16[4,72,128]{2,1,0:T(8,128)(2,1)S(1)} %pad_maximum_fusion.1), channel_id=1, source_target_pairs={{0,2},{1,3},{2,0},{3,1},{4,6},{5,7},{6,4},{7,5},{8,10},{9,11},{10,... | collective-permute-start | bytes 221192 | tf_op jit(solution)/shard_map/ppermute | solution.py:756
  13.3 2.5 %collective-permute-done.2 = bf16[4,72,128]{2,1,0:T(8,128)(2,1)S(1)} collective-permute-done((bf16[4,72,128]{2,1,0:T(8,128)(2,1)S(1)}, bf16[4,72,128]{2,1,0:T(8,128)(2,1)S(1)}, u32[]{:S(2)}, u32[]{:S(2)}) %collective-permute-start.2) | collective-permute-done | bytes 73760 | tf_op jit(solution)/shard_map/ppermute | solution.py:756
  15.8 0.1 collective-permute-start.3
  16.0 1.3 %collective-permute-done.3 = bf16[8,72,128]{2,1,0:T(8,128)(2,1)S(1)} collective-permute-done((bf16[8,72,128]{2,1,0:T(8,128)(2,1)S(1)}, bf16[8,72,128]{2,1,0:T(8,128)(2,1)S(1)}, u32[]{:S(2)}, u32[]{:S(2)}) %collective-permute-start.3) | collective-permute-done | bytes 147488 | tf_op jit(solution)/shard_map/ppermute | solution.py:756
  17.3 9.5 %strip_step.1 = (bf16[32,128]{1,0:T(8,128)(2,1)}, f32[32,128]{1,0:T(8,128)}, f32[1152,32]{1,0:T(8,128)}, f32[1152,128]{1,0:T(8,128)}, f32[32,128]{1,0:T(8,128)}, /*index=5*/f32[32,64]{1,0:T(8,128)}) custom-call(s32[3]{0:T(128)} %refs_0_.5, bf16[16,72,128]{2,1,0:T(8,128)(2,1)S(1)} %constant_dynamic-update-slice_fusion.refs_1_, ...), custom_call_target="tpu_custom_call" | custom-call | tf_op jit(solution)/shard_map/strip_step/pallas_call | solution.py:664
  (8 shorter events, 0.1 us)
Async XLA Ops:
  1.5 5.9 %collective-permute-start = (bf16[1,72,128]{2,1,0:T(8,128)(2,1)S(1)}, bf16[1,72,128]{2,1,0:T(8,128)(2,1)S(1)}, u32[]{:S(2)}, u32[]{:S(2)}) collective-permute-start(bf16[1,72,128]{2,1,0:T(8,128)(2,1)S(1)} %bitcast.9), channel_id=1, source_target_pairs={{0,8},{1,9},{2,10},{3,11},{4,12},{5,13},{6,14},{7,15},{8,0},{9,1},... | collective-permute-start | bytes 55304 | tf_op jit(solution)/shard_map/ppermute | solution.py:756
  7.4 4.0 %collective-permute-start.1 = (bf16[2,72,128]{2,1,0:T(8,128)(2,1)S(1)}, bf16[2,72,128]{2,1,0:T(8,128)(2,1)S(1)}, u32[]{:S(2)}, u32[]{:S(2)}) collective-permute-start(bf16[2,72,128]{2,1,0:T(8,128)(2,1)S(1)} %pad_maximum_fusion.2), channel_id=1, source_target_pairs={{0,4},{1,5},{2,6},{3,7},{4,0},{5,1},{6,2},{7,3},{8,12},{9,13},{10,... | collective-permute-start | bytes 110600 | tf_op jit(solution)/shard_map/ppermute | solution.py:756
  11.4 4.4 %collective-permute-start.2 = (bf16[4,72,128]{2,1,0:T(8,128)(2,1)S(1)}, bf16[4,72,128]{2,1,0:T(8,128)(2,1)S(1)}, u32[]{:S(2)}, u32[]{:S(2)}) collective-permute-start(bf16[4,72,128]{2,1,0:T(8,128)(2,1)S(1)} %pad_maximum_fusion.1), channel_id=1, source_target_pairs={{0,2},{1,3},{2,0},{3,1},{4,6},{5,7},{6,4},{7,5},{8,10},{9,11},{10,... | collective-permute-start | bytes 221192 | tf_op jit(solution)/shard_map/ppermute | solution.py:756
  15.8 1.4 %collective-permute-start.3 = (bf16[8,72,128]{2,1,0:T(8,128)(2,1)S(1)}, bf16[8,72,128]{2,1,0:T(8,128)(2,1)S(1)}, u32[]{:S(2)}, u32[]{:S(2)}) collective-permute-start(bf16[8,72,128]{2,1,0:T(8,128)(2,1)S(1)} %pad_maximum_fusion), channel_id=1, source_target_pairs={{0,1},{1,0},{2,3},{3,2},{4,5},{5,4},{6,7},{7,6},{8,9},{9,8},{10,11... | collective-permute-start | bytes 442376 | tf_op jit(solution)/shard_map/ppermute | solution.py:756
